TPU v7x, 32 devices: a whole 2x2x4 slice. The times are simulated.
32 devices in a mesh: fsdp: 16 (over z, y, x), tp: 2 (over core).
Axes of the slice: x: 2, y: 2, z: 4, core: 2. Of those that a mesh axis runs over, the one named last changes fastest.
Arguments:
- tokens: bfloat16 [4096, 896], P(('fsdp', 'tp')), may hold values from -6 to 6
- cotangent: bfloat16 [4096, 896], P(('fsdp', 'tp')), may hold values from -6 to 6
- parents: int32 [16, 2], P('fsdp'), may hold values from 0 to 0, as said below
- skip: int32 [16], P('fsdp'), may hold values 0 or 1
- w_query: bfloat16 [896, 896], P('fsdp', 'tp'), may hold values from -0.1875 to 0.1875
- key_matrix: bfloat16 [896, 128], P('fsdp', 'tp'), may hold values from -0.1875 to 0.1875
- value_matrix: bfloat16 [896, 128], P('fsdp', 'tp'), may hold values from -0.1875 to 0.1875
- w_out: bfloat16 [896, 896], P('tp', 'fsdp'), may hold values from -0.75 to 0.75
- w_gate: bfloat16 [896, 4864], P('fsdp', 'tp'), may hold values from -0.1875 to 0.1875
- w_up: bfloat16 [896, 4864], P('fsdp', 'tp'), may hold values from -0.1875 to 0.1875
- w_down: bfloat16 [4864, 896], P('tp', 'fsdp'), may hold values from -0.078125 to 0.078125
- gain_attn: bfloat16 [896], P('fsdp'), may hold values from 0.5 to 1.5
- gain_mlp: bfloat16 [896], P('fsdp'), may hold values from 0.5 to 1.5
Outputs:
- output: bfloat16 [4096, 896], P(('fsdp', 'tp'))
- grad_tokens: bfloat16 [4096, 896], P(('fsdp', 'tp'))
- grad_w_query: float32 [896, 896], P('fsdp', 'tp')
- grad_w_key: float32 [896, 128], P('fsdp', 'tp')
- grad_w_value: float32 [896, 128], P('fsdp', 'tp')
- grad_w_out: float32 [896, 896], P('tp', 'fsdp')
- grad_w_gate: float32 [896, 4864], P('fsdp', 'tp')
- grad_w_up: float32 [896, 4864], P('fsdp', 'tp')
- grad_w_down: float32 [4864, 896], P('tp', 'fsdp')
- grad_gain_attn: float32 [896], P('fsdp')
- grad_gain_mlp: float32 [896], P('fsdp')
Inputs may be any that keep to these rules, and one draw needn't show every extreme that they name: `parents`: block 0 of a tree is its own parent; each tree has two blocks, and block 1 has block 0 as its parent, so every tree's mask is causal and pos is the token's place in its tree.
All inputs are finite; a program needn't handle non-finite values. No bound on the sum of `skip` on one device may be relied on, other than what follows from the above.
Results may differ from a plain program's by a relative error of at most 0.015.
Values may be sent and summed in bfloat16 or wider, within the bound.
No kernel may reach another device: no remote copies, remote signals or barrier semaphores. Data moves between devices by JAX's collectives and lax.ppermute only.
A program may use at most 192 MiB of HBM per device.

v0:
```python
import jax
import jax.numpy as jnp
from jax import lax
from jax.sharding import PartitionSpec as P

HEAD_SIZE = 64
BLK = 128


eps = 1e-05
rotary_base = 10000.0


def cut_along(value, dim, peers):
    shape = value.shape
    pieces = value.reshape(*shape[:dim], peers, shape[dim] // peers, *shape[dim + 1 :])
    return jnp.moveaxis(pieces, dim, 0)


def summed_on_arrival(value, axis, dim):
    peers = lax.axis_size(axis)
    pieces = lax.all_to_all(cut_along(value, dim, peers), axis, 0, 0, tiled=True)
    return jnp.sum(pieces.astype(jnp.float32), axis=0)


def tree_tables(parents, blocks, block_len):
    block_ids = jnp.arange(blocks, dtype=jnp.int32)
    ancestry = jnp.eye(blocks, dtype=jnp.float32)
    depths = jnp.zeros((blocks,), jnp.float32)
    picked = (block_ids == parents[1]).astype(jnp.float32)
    inherited = jnp.sum(picked[:, None] * ancestry, axis=0)
    ancestry = ancestry.at[1].set(jnp.maximum(ancestry[1], inherited))
    depths = depths.at[1].set(jnp.sum(picked * depths) + 1.0)
    token_ids = jnp.arange(blocks * block_len, dtype=jnp.int32)
    spread = jnp.repeat(jnp.repeat(ancestry, block_len, axis=0), block_len, axis=1)
    visible = (spread > 0.5) & (token_ids[None, :] <= token_ids[:, None])
    token_position = jnp.repeat(depths, block_len) * block_len + (token_ids % block_len).astype(
        jnp.float32
    )
    return (visible, token_position)


def apply_rotation(values, token_position, head_count, direction):
    count_of_rows = values.shape[0]
    shaped = values.reshape(count_of_rows, head_count, HEAD_SIZE)
    half_size = HEAD_SIZE // 2
    frequency = rotary_base ** (-2.0 * jnp.arange(half_size, dtype=jnp.float32) / HEAD_SIZE)
    angles = token_position[:, None] * frequency[None, :]
    cosine = jnp.cos(angles)[:, None, :]
    sine_part = direction * jnp.sin(angles)[:, None, :]
    first_half = shaped[..., :half_size]
    second_half = shaped[..., half_size:]
    turned = jnp.concatenate(
        [
            first_half * cosine - second_half * sine_part,
            second_half * cosine + first_half * sine_part,
        ],
        axis=-1,
    )
    return turned.reshape(count_of_rows, head_count * HEAD_SIZE)


def fetch_attention(w_query, key_matrix, value_matrix, w_out, gain_attn):
    return (
        lax.all_gather(w_query, "fsdp", axis=0, tiled=True),
        lax.all_gather(key_matrix, "fsdp", axis=0, tiled=True),
        lax.all_gather(value_matrix, "fsdp", axis=0, tiled=True),
        lax.all_gather(w_out, "fsdp", axis=1, tiled=True),
        lax.all_gather(gain_attn, "fsdp", axis=0, tiled=True),
    )


def fetch_mlp(w_gate, w_up, w_down, gain_mlp):
    return (
        lax.all_gather(w_gate, "fsdp", axis=0, tiled=True),
        lax.all_gather(w_up, "fsdp", axis=0, tiled=True),
        lax.all_gather(w_down, "fsdp", axis=1, tiled=True),
        lax.all_gather(gain_mlp, "fsdp", axis=0, tiled=True),
    )


def rows_inner(first_array, second_array):
    return lax.dot_general(
        first_array, second_array, (((0,), (0,)), ((), ())), preferred_element_type=jnp.float32
    )


def against(first_array, second_array):
    return lax.dot_general(
        first_array, second_array, (((1,), (1,)), ((), ())), preferred_element_type=jnp.float32
    )


def norm_back(grad_normed, scaled, statistic, gain_vector):
    grad_scaled = grad_normed * gain_vector
    return statistic * (
        grad_scaled - scaled * jnp.mean(grad_scaled * scaled, axis=-1, keepdims=True)
    )


def on_device(
    tokens,
    cotangent,
    parents,
    skip,
    w_query,
    key_matrix,
    value_matrix,
    w_out,
    w_gate,
    w_up,
    w_down,
    gain_attn,
    gain_mlp,
):
    half_rows = tokens.shape[0]
    seq_len = half_rows * lax.axis_size("tp")
    blocks = seq_len // BLK
    shard_rows = w_query.shape[0]
    heads_here = w_query.shape[1] // HEAD_SIZE
    kv_here = key_matrix.shape[1] // HEAD_SIZE
    heads_per_group = heads_here // kv_here
    query_cols = heads_here * HEAD_SIZE
    kv_cols = kv_here * HEAD_SIZE
    ff_here = w_gate.shape[1]
    score_scale = HEAD_SIZE ** (-0.5)
    visible, token_position = tree_tables(parents[0], blocks, BLK)
    active = (1 - skip[0]).astype(jnp.float32)
    query_all, key_all, value_all, out_all, gain_one = fetch_attention(
        w_query, key_matrix, value_matrix, w_out, gain_attn
    )
    inputs = tokens.astype(jnp.float32)
    stat_one = lax.rsqrt(jnp.mean(inputs * inputs, axis=-1, keepdims=True) + eps)
    scaled_one = inputs * stat_one
    gain_one_wide = gain_one.astype(jnp.float32)
    normed_input = (scaled_one * gain_one_wide).astype(jnp.bfloat16)
    normed_all = lax.all_gather(normed_input, "tp", axis=0, tiled=True)
    query_rows = apply_rotation(
        jnp.dot(normed_all, query_all, preferred_element_type=jnp.float32),
        token_position,
        heads_here,
        1.0,
    ).astype(jnp.bfloat16)
    key_row_block = apply_rotation(
        jnp.dot(normed_all, key_all, preferred_element_type=jnp.float32),
        token_position,
        kv_here,
        1.0,
    ).astype(jnp.bfloat16)
    value_row_block = jnp.dot(normed_all, value_all, preferred_element_type=jnp.float32).astype(
        jnp.bfloat16
    )
    query_per_head = query_rows.reshape(seq_len, kv_here, heads_per_group, HEAD_SIZE)
    key_per_head = key_row_block.reshape(seq_len, kv_here, HEAD_SIZE)
    value_per_head = value_row_block.reshape(seq_len, kv_here, HEAD_SIZE)

    def score_table():
        raw_scores = (
            jnp.einsum(
                "qhgd,khd->hgqk", query_per_head, key_per_head, preferred_element_type=jnp.float32
            )
            * score_scale
        )
        return jnp.where(visible, raw_scores, -1e30)

    scores = score_table()
    row_max = jnp.max(scores, axis=-1, keepdims=True)
    exponent = jnp.exp(scores - row_max)
    row_total = jnp.sum(exponent, axis=-1, keepdims=True)
    log_total = row_max + jnp.log(row_total)
    probs_low = (exponent / row_total).astype(jnp.bfloat16)
    attended = jnp.einsum(
        "hgqk,khd->qhgd", probs_low, value_per_head, preferred_element_type=jnp.float32
    )
    attended = attended.reshape(seq_len, query_cols).astype(jnp.bfloat16)
    branch = lax.psum_scatter(
        jnp.dot(attended, out_all, preferred_element_type=jnp.float32).astype(jnp.bfloat16),
        "tp",
        scatter_dimension=0,
        tiled=True,
    ).astype(jnp.float32)
    middle = inputs + active * branch
    gate_all, up_all, down_all, gain_two = fetch_mlp(w_gate, w_up, w_down, gain_mlp)
    stat_two = lax.rsqrt(jnp.mean(middle * middle, axis=-1, keepdims=True) + eps)
    scaled_two = middle * stat_two
    gain_two_wide = gain_two.astype(jnp.float32)
    normed_mlp = (scaled_two * gain_two_wide).astype(jnp.bfloat16)
    normed_mlp_all = lax.all_gather(normed_mlp, "tp", axis=0, tiled=True)
    gate_sum = jnp.dot(normed_mlp_all, gate_all, preferred_element_type=jnp.float32)
    upward = jnp.dot(normed_mlp_all, up_all, preferred_element_type=jnp.float32)
    sigmoid_gate = jax.nn.sigmoid(gate_sum)
    hidden = (gate_sum * sigmoid_gate * upward).astype(jnp.bfloat16)
    mlp_result = lax.psum_scatter(
        jnp.dot(hidden, down_all, preferred_element_type=jnp.float32).astype(jnp.bfloat16),
        "tp",
        scatter_dimension=0,
        tiled=True,
    ).astype(jnp.float32)
    output = (middle + active * mlp_result).astype(jnp.bfloat16)
    grad_out = cotangent.astype(jnp.float32)
    grad_mlp = (active * grad_out).astype(jnp.bfloat16)
    grad_mlp_all = lax.all_gather(grad_mlp, "tp", axis=0, tiled=True)
    gate_all, up_all, down_all, gain_two = fetch_mlp(w_gate, w_up, w_down, gain_mlp)
    gain_two_wide = gain_two.astype(jnp.float32)
    grad_hidden = against(grad_mlp_all, down_all)
    grad_gate = (
        grad_hidden * upward * sigmoid_gate * (1.0 + gate_sum * (1.0 - sigmoid_gate))
    ).astype(jnp.bfloat16)
    grad_up = (grad_hidden * gate_sum * sigmoid_gate).astype(jnp.bfloat16)
    grad_normed_mlp = lax.psum_scatter(
        (against(grad_gate, gate_all) + against(grad_up, up_all)).astype(jnp.bfloat16),
        "tp",
        scatter_dimension=0,
        tiled=True,
    ).astype(jnp.float32)
    column_part = normed_mlp_all
    grad_part = grad_mlp_all
    mlp_grads = lax.psum_scatter(
        jnp.concatenate(
            [
                rows_inner(column_part, grad_gate),
                rows_inner(column_part, grad_up),
                rows_inner(grad_part, hidden),
            ],
            axis=1,
        ),
        "fsdp",
        scatter_dimension=0,
        tiled=True,
    )
    grad_gain_two = jnp.sum(grad_normed_mlp * scaled_two, axis=0)
    grad_middle = grad_out + norm_back(grad_normed_mlp, scaled_two, stat_two, gain_two_wide)
    grad_branch = (active * grad_middle).astype(jnp.bfloat16)
    grad_branch_all = lax.all_gather(grad_branch, "tp", axis=0, tiled=True)
    query_all, key_all, value_all, out_all, gain_one = fetch_attention(
        w_query, key_matrix, value_matrix, w_out, gain_attn
    )
    gain_one_wide = gain_one.astype(jnp.float32)
    grad_attended = (
        against(grad_branch_all, out_all)
        .astype(jnp.bfloat16)
        .reshape(seq_len, kv_here, heads_per_group, HEAD_SIZE)
    )
    probs = jnp.exp(score_table() - log_total)
    probs_low = probs.astype(jnp.bfloat16)
    grad_probs = jnp.einsum(
        "qhgd,khd->hgqk", grad_attended, value_per_head, preferred_element_type=jnp.float32
    )
    grad_value = jnp.einsum(
        "hgqk,qhgd->khd", probs_low, grad_attended, preferred_element_type=jnp.float32
    )
    grad_value = grad_value.reshape(seq_len, kv_cols).astype(jnp.bfloat16)
    grad_scores = (
        probs * (grad_probs - jnp.sum(probs * grad_probs, axis=-1, keepdims=True))
    ).astype(jnp.bfloat16)
    grad_query = (
        jnp.einsum(
            "hgqk,khd->qhgd", grad_scores, key_per_head, preferred_element_type=jnp.float32
        ).reshape(seq_len, query_cols)
        * score_scale
    )
    grad_key = (
        jnp.einsum(
            "hgqk,qhgd->khd", grad_scores, query_per_head, preferred_element_type=jnp.float32
        ).reshape(seq_len, kv_cols)
        * score_scale
    )
    grad_query = apply_rotation(grad_query, token_position, heads_here, -1.0).astype(jnp.bfloat16)
    grad_key = apply_rotation(grad_key, token_position, kv_here, -1.0).astype(jnp.bfloat16)
    first_term = against(grad_query, query_all)
    second_term = against(grad_key, key_all)
    third_term = against(grad_value, value_all)
    grad_normed = lax.psum_scatter(
        (first_term + second_term + third_term).astype(jnp.bfloat16),
        "tp",
        scatter_dimension=0,
        tiled=True,
    ).astype(jnp.float32)
    column_part = normed_all
    grad_part = grad_branch_all
    attn_grads = summed_on_arrival(
        jnp.concatenate(
            [
                rows_inner(column_part, grad_query),
                rows_inner(column_part, grad_key),
                rows_inner(column_part, grad_value),
                rows_inner(grad_part, attended),
            ],
            axis=1,
        ).astype(jnp.bfloat16),
        "fsdp",
        0,
    )
    grad_gain_one = jnp.sum(grad_normed * scaled_one, axis=0)
    grad_tokens = (
        grad_middle + norm_back(grad_normed, scaled_one, stat_one, gain_one_wide)
    ).astype(jnp.bfloat16)
    gain_total_one, gain_total_two = lax.psum((grad_gain_one, grad_gain_two), ("fsdp", "tp"))
    offset = lax.axis_index("fsdp") * shard_rows
    grad_gain_attn = lax.dynamic_slice_in_dim(gain_total_one, offset, shard_rows)
    grad_gain_mlp = lax.dynamic_slice_in_dim(gain_total_two, offset, shard_rows)
    grad_w_query = attn_grads[:, :query_cols]
    grad_w_key = attn_grads[:, query_cols : query_cols + kv_cols]
    grad_w_value = attn_grads[:, query_cols + kv_cols : query_cols + 2 * kv_cols]
    grad_w_out = attn_grads[:, query_cols + 2 * kv_cols :].T
    grad_w_gate = mlp_grads[:, :ff_here]
    grad_w_up = mlp_grads[:, ff_here : 2 * ff_here]
    grad_w_down = mlp_grads[:, 2 * ff_here :].T
    return (
        output,
        grad_tokens,
        grad_w_query,
        grad_w_key,
        grad_w_value,
        grad_w_out,
        grad_w_gate,
        grad_w_up,
        grad_w_down,
        grad_gain_attn,
        grad_gain_mlp,
    )


def solution(mesh):
    in_specs = (
        P(("fsdp", "tp"), None),
        P(("fsdp", "tp"), None),
        P("fsdp", None),
        P("fsdp"),
        P("fsdp", "tp"),
        P("fsdp", "tp"),
        P("fsdp", "tp"),
        P("tp", "fsdp"),
        P("fsdp", "tp"),
        P("fsdp", "tp"),
        P("tp", "fsdp"),
        P("fsdp"),
        P("fsdp"),
    )
    out_specs = (
        P(("fsdp", "tp"), None),
        P(("fsdp", "tp"), None),
        P("fsdp", "tp"),
        P("fsdp", "tp"),
        P("fsdp", "tp"),
        P("tp", "fsdp"),
        P("fsdp", "tp"),
        P("fsdp", "tp"),
        P("tp", "fsdp"),
        P("fsdp"),
        P("fsdp"),
    )
    return jax.shard_map(
        on_device, mesh=mesh, in_specs=in_specs, out_specs=out_specs, check_vma=False
    )
```

profile of v0, /device:TPU:0, one launch (start us, length us, event | category | flops | bytes accessed | tf_op | source)
XLA Modules:
  0.0 1254.3 jit_solution(5714153399740913930)
XLA Ops:
  8.1 1.2 slice.77
  10.1 1.1 fusion.34
  11.5 1.3 fusion.70
  13.4 0.8 dynamic-update-slice.6
  14.3 0.8 dynamic-update-slice.5
  15.1 44.2 %all-reduce.4 = (bf16[896]{0:T(1024)(128)(2,1)}, bf16[896]{0:T(1024)(128)(2,1)S(1)}) all-reduce(bf16[896]{0:T(1024)(128)(2,1)S(1)} %dynamic-update-slice.6, bf16[896]{0:T(1024)(128)(2,1)S(1)} %dynamic-update-slice.5), channel_id=1, replica_groups=mesh['fsdp'=16,'tp'=2] {'fsdp'}, use_global_device_ids=true, to_apply=%add.1 | all-reduce | flops 1792 | bytes 7168
  59.4 37.0 %all_gather.51 = bf16[896,64]{1,0:T(8,128)(2,1)S(1)} all-gather(bf16[56,64]{1,0:T(8,128)(2,1)} %param.22), channel_id=1, replica_groups=mesh['fsdp'=16,'tp'=2] {'fsdp'}, dimensions={0}, use_global_device_ids=true | all-gather | bytes 121856 | tf_op jit(solution)/shard_map/all_gather | solution.py:66
  96.4 38.9 %all_gather.50 = bf16[896,64]{1,0:T(8,128)(2,1)S(1)} all-gather(bf16[56,64]{1,0:T(8,128)(2,1)} %param.23), channel_id=1, replica_groups=mesh['fsdp'=16,'tp'=2] {'fsdp'}, dimensions={0}, use_global_device_ids=true | all-gather | bytes 121856 | tf_op jit(solution)/shard_map/all_gather | solution.py:67
  135.3 1.1 fusion.31
  136.5 2.1 all_gather.49
  139.2 0.8 broadcast_multiply_fusion
  140.3 40.7 %all_gather.52 = bf16[896,448]{1,0:T(8,128)(2,1)S(1)} all-gather(bf16[56,448]{1,0:T(8,128)(2,1)S(1)} %copy-done.37), channel_id=1, replica_groups=mesh['fsdp'=16,'tp'=2] {'fsdp'}, dimensions={0}, use_global_device_ids=true | all-gather | bytes 852992 | tf_op jit(solution)/shard_map/all_gather | solution.py:65
  181.5 43.4 %all_gather.53 = bf16[448,896]{0,1:T(8,128)(2,1)S(1)} all-gather(bf16[448,56]{0,1:T(8,128)(2,1)S(1)} %copy-done.38), channel_id=1, replica_groups=mesh['fsdp'=16,'tp'=2] {'fsdp'}, dimensions={1}, use_global_device_ids=true | all-gather | bytes 852992 | tf_op jit(solution)/shard_map/all_gather | solution.py:68
  226.4 0.7 copy-done.18
  227.1 1.2 convolution_convert_fusion.3
  230.8 1.3 convert_element_type.213
  232.1 1.0 fusion.29
  233.1 2.3 all_gather.59
  235.3 1.3 log_add_fusion
  236.7 1.1 multiply_reduce_fusion
  238.4 1.1 multiply_convert_fusion.4
  239.4 2.3 all_gather.55
  241.7 63.3 %all-gather.6.cloned.1.call-done = bf16[896,2432]{1,0:T(8,128)(2,1)} async-done(((bf16[56,2432]{1,0:T(8,128)(2,1)}), bf16[896,2432]{1,0:T(8,128)(2,1)}) %all-gather.6.cloned.1.call-update) | async-done | bytes 4358160 | tf_op jit(solution)/shard_map/all_gather | solution.py:76
  305.1 5.3 fusion.74
  310.4 73.4 %all-gather.4.cloned.1.call-done = bf16[896,2432]{1,0:T(8,128)(2,1)} async-done(((bf16[56,2432]{1,0:T(8,128)(2,1)}), bf16[896,2432]{1,0:T(8,128)(2,1)}) %all-gather.4.cloned.1.call-update) | async-done | bytes 4358160 | tf_op jit(solution)/shard_map/all_gather | solution.py:75
  383.7 5.3 fusion.73
  389.1 73.4 %all-gather.8.cloned.1.call-done = bf16[2432,896]{0,1:T(8,128)(2,1)} async-done(((bf16[2432,56]{0,1:T(8,128)(2,1)}), bf16[2432,896]{0,1:T(8,128)(2,1)}) %all-gather.8.cloned.1.call-update) | async-done | bytes 4358160 | tf_op jit(solution)/shard_map/all_gather | solution.py:77
  462.4 6.9 multiply_convert_fusion
  469.3 1.5 fusion.75
  470.9 4.6 fusion.6
  475.7 6.3 fusion.78
  482.0 4.8 fusion.77
  486.9 2.0 fusion.30
  488.9 1.4 multiply_convert_fusion.3
  490.3 2.1 all_gather.60
  496.9 1.1 fusion.5
  498.1 4.6 convolution_convert_fusion.2
  502.7 4.8 fusion.79
  507.6 19.7 %pad_maximum_fusion = f32[896,7296]{1,0:T(8,128)} fusion(f32[896,2432]{1,0:T(8,128)} %fusion.79, f32[896,2432]{1,0:T(8,128)} %fusion.78, f32[896,2432]{1,0:T(8,128)} %fusion.77), kind=kLoop, calls=%fused_computation | loop fusion | flops 13074432 | bytes 52297728 | tf_op jit(solution)/shard_map/concatenate | solution.py:219
  527.5 0.8 copy-done.6
  529.9 2.1 pad_maximum_fusion.1
  532.0 4.4 all-to-all-start
  537.2 1.2 fusion.33
  538.4 106.9 %all-reduce.3 = (f32[896]{0:T(1024)S(1)}, f32[896]{0:T(1024)S(1)}) all-reduce(f32[896]{0:T(1024)S(1)} %get-tuple-element.37, f32[896]{0:T(1024)S(1)} %copy-done.41), channel_id=1, replica_groups=mesh['fsdp'=16,'tp'=2] {'fsdp','tp'}, use_global_device_ids=true, to_apply=%region_15.16 | all-reduce | flops 1792 | bytes 14336 | tf_op jit(solution)/shard_map/psum | solution.py:298
  646.6 2.2 fusion.26
  649.8 0.7 slice_bitcast_fusion
  650.5 593.5 %all-reduce.7.cloned.1.call-done = f32[896,7296]{1,0:T(8,128)} async-done(((f32[896,7296]{1,0:T(8,128)}), f32[896,7296]{1,0:T(8,128)}) %all-reduce.7.cloned.1.call-update) | async-done | bytes 26148880
  1244.0 2.9 dynamic-slice_bitcast_fusion
  (173 shorter events, 14.8 us)
Async XLA Ops:
  8.0 228.6 %reduce-scatter.5.cloned.1.call-start = ((), (), s32[]{:S(2)}) async-start(), calls=%async_computation.5 | async-start | bytes 688128 | tf_op jit(solution)/shard_map/reduce_scatter | solution.py:176
  8.1 131.9 %copy-start.46 = (f32[32]{0:T(128)}, f32[32]{0:T(128)S(1)}, u32[]{:S(2)}) copy-start(f32[32]{0:T(128)S(1)} %multiply_power_fusion) | copy-start | bytes 388
  8.1 131.9 %copy-start.42 = (f32[256]{0:T(256)}, f32[256]{0:T(256)S(1)}, u32[]{:S(2)}) copy-start(f32[256]{0:T(256)S(1)} %fusion.62) | copy-start | bytes 3076
  10.1 130.1 %copy-start.37 = (bf16[56,448]{1,0:T(8,128)(2,1)S(1)}, bf16[56,448]{1,0:T(8,128)(2,1)}, u32[]{:S(2)}) copy-start(bf16[56,448]{1,0:T(8,128)(2,1)} %param.21) | copy-start | bytes 150532
  11.2 124.1 %copy-start.48 = (f32[128]{0:T(128)}, f32[128]{0:T(128)S(1)}, u32[]{:S(2)}) copy-start(f32[128]{0:T(128)S(1)} %add_rsqrt_fusion.1) | copy-start | bytes 1540
  59.3 76.0 %copy-start.31 = (f32[896]{0:T(1024)}, f32[896]{0:T(1024)S(1)}, u32[]{:S(2)}) copy-start(f32[896]{0:T(1024)S(1)} %convert_element_type.200) | copy-start | bytes 10756
  96.4 43.6 %copy-start.12 = (bf16[896,64]{1,0:T(8,128)(2,1)}, bf16[896,64]{1,0:T(8,128)(2,1)S(1)}, u32[]{:S(2)}) copy-start(bf16[896,64]{1,0:T(8,128)(2,1)S(1)} %all_gather.51) | copy-start | bytes 344068
  135.3 45.7 %copy-start.10 = (bf16[896,64]{1,0:T(8,128)(2,1)}, bf16[896,64]{1,0:T(8,128)(2,1)S(1)}, u32[]{:S(2)}) copy-start(bf16[896,64]{1,0:T(8,128)(2,1)S(1)} %all_gather.50) | copy-start | bytes 344068
  138.9 86.9 %copy-start.27 = (bf16[256,64,1]{0,1,2:T(8,128)(2,1)}, bf16[256,64,1]{0,1,2:T(8,128)(2,1)S(1)}, u32[]{:S(2)}) copy-start(bf16[256,64,1]{0,1,2:T(8,128)(2,1)S(1)} %fusion.11) | copy-start | bytes 98308
  138.9 42.6 %copy-start.38 = (bf16[448,56]{0,1:T(8,128)(2,1)S(1)}, bf16[448,56]{0,1:T(8,128)(2,1)}, u32[]{:S(2)}) copy-start(bf16[448,56]{0,1:T(8,128)(2,1)} %param.24) | copy-start | bytes 150532
  140.0 84.9 %copy-start.24 = (f32[256,32]{0,1:T(8,128)}, f32[256,32]{0,1:T(8,128)S(1)}, u32[]{:S(2)}) copy-start(f32[256,32]{0,1:T(8,128)S(1)} %get-tuple-element.65) | copy-start | bytes 98308
  140.2 84.7 %copy-start.33 = (bf16[256,32]{0,1:T(8,128)(2,1)}, bf16[256,32]{0,1:T(8,128)(2,1)S(1)}, u32[]{:S(2)}) copy-start(bf16[256,32]{0,1:T(8,128)(2,1)S(1)} %get-tuple-element.61) | copy-start | bytes 49156
  140.2 84.7 %copy-start.35 = (bf16[256,32]{0,1:T(8,128)(2,1)}, bf16[256,32]{0,1:T(8,128)(2,1)S(1)}, u32[]{:S(2)}) copy-start(bf16[256,32]{0,1:T(8,128)(2,1)S(1)} %get-tuple-element.62) | copy-start | bytes 49156
  224.9 1.5 copy-start.1
  227.1 9.6 copy-start
  228.3 76.7 %all-gather.6.cloned.1.call-start = ((), (), s32[]{:S(2)}) async-start(), calls=%async_computation.7 | async-start | bytes 4630528 | tf_op jit(solution)/shard_map/all_gather | solution.py:76
  228.9 154.8 %all-gather.4.cloned.1.call-start = ((), (), s32[]{:S(2)}) async-start(), calls=%async_computation.6 | async-start | bytes 4630528 | tf_op jit(solution)/shard_map/all_gather | solution.py:75
  229.5 232.9 %all-gather.8.cloned.1.call-start = ((), (), s32[]{:S(2)}) async-start(), calls=%async_computation.8 | async-start | bytes 4630528 | tf_op jit(solution)/shard_map/all_gather | solution.py:77
  230.1 256.8 %reduce-scatter.9.cloned.1.call-start = ((), (), s32[]{:S(2)}) async-start(), calls=%async_computation.10 | async-start | bytes 688128 | tf_op jit(solution)/shard_map/reduce_scatter | solution.py:210
  462.4 6.9 copy-start.52
  469.3 1.6 copy-start.15
  469.3 1.6 copy-start.17
  475.5 61.7 %reduce-scatter.11.cloned.1.call-start = ((), (), s32[]{:S(2)}) async-start(), calls=%async_computation.11 | async-start | bytes 688128 | tf_op jit(solution)/shard_map/reduce_scatter | solution.py:273
  475.7 6.3 copy-start.3
  475.7 6.3 copy-start.16
  486.9 5.6 copy-start.2
  488.9 4.1 copy-start.26
  488.9 1.4 copy-start.50
  493.4 3.4 copy-start.22
  493.9 1.3 copy-start.34
  493.9 1.3 copy-start.36
  496.5 1.5 copy-start.14
  498.0 148.5 %reduce-scatter.7.cloned.1.call-start = ((), (), s32[]{:S(2)}) async-start(), calls=%async_computation.9 | async-start | bytes 688128 | tf_op jit(solution)/shard_map/reduce_scatter | solution.py:193
  498.1 4.6 copy-start.7
  507.5 736.5 %all-reduce.7.cloned.1.call-start = ((), (), s32[]{:S(2)}) async-start(), calls=%async_computation.12 | async-start | bytes 52297728
  527.3 1.0 copy-start.6
  527.3 1.5 copy-start.23
  528.3 1.2 copy-start.19
  532.0 5.2 copy-start.32
  532.0 5.2 copy-start.49
  532.0 6.4 copy-start.41
  532.0 114.5 %copy-start.4 = (bf16[128,896]{1,0:T(8,128)(2,1)S(1)}, bf16[128,896]{1,0:T(8,128)(2,1)}, u32[]{:S(2)}) copy-start(bf16[128,896]{1,0:T(8,128)(2,1)} %reduce-scatter.5.cloned.1.call-done) | copy-start | bytes 688132
  532.0 114.5 %copy-start.8 = (bf16[128,896]{1,0:T(8,128)(2,1)S(1)}, bf16[128,896]{1,0:T(8,128)(2,1)}, u32[]{:S(2)}) copy-start(bf16[128,896]{1,0:T(8,128)(2,1)} %param.18) | copy-start | bytes 688132
  532.0 114.5 %copy-start.9 = (bf16[128,896]{1,0:T(8,128)(2,1)S(1)}, bf16[128,896]{1,0:T(8,128)(2,1)}, u32[]{:S(2)}) copy-start(bf16[128,896]{1,0:T(8,128)(2,1)} %reduce-scatter.9.cloned.1.call-done) | copy-start | bytes 688132
  532.0 114.5 %copy-start.30 = (f32[896]{0:T(1024)S(1)}, f32[896]{0:T(1024)}, u32[]{:S(2)}) copy-start(f32[896]{0:T(1024)} %convert_element_type.213) | copy-start | bytes 10756
  532.0 114.5 %copy-start.45 = (f32[128]{0:T(128)S(1)}, f32[128]{0:T(128)}, u32[]{:S(2)}) copy-start(f32[128]{0:T(128)} %copy-done.44) | copy-start | bytes 1540
  532.0 114.5 %copy-start.51 = (f32[128]{0:T(128)S(1)}, f32[128]{0:T(128)}, u32[]{:S(2)}) copy-start(f32[128]{0:T(128)} %copy-done.50) | copy-start | bytes 1540
  532.0 116.7 %all-to-all-start = ((bf16[16,56,1024]{2,1,0:T(8,128)(2,1)}), bf16[16,56,1024]{2,1,0:T(8,128)(2,1)S(1)}, u32[]{:S(2)}, u32[]{:S(2)}) async-start(bf16[16,56,1024]{2,1,0:T(8,128)(2,1)} %pad_maximum_fusion.1), calls=%async_computation.4 | async-start | bytes 3670016 | tf_op jit(solution)/shard_map/all_to_all | solution.py:22
  (14 other events, 11.7 us)
Sparse Core Ops, SparseCore 0:
  228.5 3.9 reduce-scatter.4
  475.6 6.4 reduce-scatter.8
  498.1 6.5 reduce-scatter.10
  507.6 8.8 reduce-scatter.6
Sparse Core Ops, SparseCore 1:
  231.9 73.1 all-gather.5
  308.0 75.7 all-gather.3
  386.7 75.7 all-gather.7
  527.4 716.6 all-reduce.6
where the time goes:
time: 1260 us; the launch traced here: 1250 us
  waiting for transfers between devices  805 us (64%)
  blocking collectives  320 us (25%)
  matrix products  52.7 us (4%)
  other arithmetic  39.9 us (3%)
  between operations  18.2 us (1%)
  local copies, waits for them, and re-layouts  13.3 us (1%)
    unnamed x9, waiting for transfers between devices  595 us
    psum x1, blocking collectives, on_device(): lax.psum((grad_gain_one, grad_gain_two), ('fsdp', 'tp'))  107 us
    all_gather x1, waiting for transfers between devices, fetch_mlp(): lax.all_gather(w_gate, 'fsdp', axis=0, tiled=True)  73.4 us
    all_gather x1, waiting for transfers between devices, fetch_mlp(): lax.all_gather(w_down, 'fsdp', axis=1, tiled=True)  73.4 us
    all_gather x1, waiting for transfers between devices, fetch_mlp(): lax.all_gather(w_up, 'fsdp', axis=0, tiled=True)  63.3 us
    unnamed x1, blocking collectives  44.2 us
    all_gather x1, blocking collectives, fetch_attention(): lax.all_gather(w_out, 'fsdp', axis=1, tiled=True)  43.4 us
    all_gather x1, blocking collectives, fetch_attention(): lax.all_gather(w_query, 'fsdp', axis=0, tiled=True)  40.7 us
  transfers between devices with their start and end apart: 9, of which 4 were waited for; matrix products, arithmetic and copies ran while one was open for 5% of the time, Pallas kernels for 0%

commit v1 on v0

v1 whole, which is shorter than its diff:
```python
import jax
import jax.numpy as jnp
import numpy as np
from jax import lax
from jax.sharding import Mesh, PartitionSpec as P

HEAD_SIZE = 64
LANES = 128
eps = 1e-05
rotary_base = 10000.0
bf16 = jnp.bfloat16
f32 = jnp.float32
T_AXES = ("z0", "x")
SWAP = [(0, 1), (1, 0)]


def rotary_tables(seq_len, heads):
    half = HEAD_SIZE // 2
    frequency = rotary_base ** (-2.0 * np.arange(half, dtype=np.float32) / HEAD_SIZE)
    angles = np.arange(seq_len, dtype=np.float32)[:, None] * frequency[None, :].astype(np.float32)
    return np.cos(angles).astype(np.float32), np.sin(angles).astype(np.float32)


def rotate(values, cosine, sine):
    rows = values.shape[0]
    half = HEAD_SIZE // 2
    shaped = values.reshape(rows, -1, HEAD_SIZE)
    a = shaped[..., :half]
    b = shaped[..., half:]
    c = cosine[:, None, :]
    s = sine[:, None, :]
    return jnp.concatenate([a * c - b * s, b * c + a * s], axis=-1).reshape(rows, -1)


def nn(a, b):
    return lax.dot_general(a, b, (((1,), (0,)), ((), ())), preferred_element_type=f32)


def tn(a, b):
    return lax.dot_general(a, b, (((0,), (0,)), ((), ())), preferred_element_type=f32)


def nt(a, b):
    return lax.dot_general(a, b, (((1,), (1,)), ((), ())), preferred_element_type=f32)


def swap(value, axis):
    return lax.ppermute(value, axis, SWAP)


def spread(value, axes):
    peers = 1
    for axis in axes:
        peers *= lax.axis_size(axis)
    wide = jnp.broadcast_to(value[None], (peers,) + value.shape)
    return lax.all_to_all(wide, axes, 0, 0, tiled=True)


def t_partner(x_bit, z_bit):
    return [
        (i, (((i // 2) ^ z_bit) * 2) + ((i % 2) ^ x_bit)) for i in range(4)
    ]


def t_send(values):
    return [
        lax.ppermute(v, T_AXES, t_partner(xb, zb))
        for v, (xb, zb) in zip(values, ((1, 0), (0, 1), (1, 1)))
    ]


def share_tokens(own_half):
    got = jnp.stack([own_half] + t_send([own_half] * 3))
    other = swap(got, "tp")
    return jnp.stack([got, other], axis=1)


def return_tokens(partial):
    away = partial[:, 1].astype(bf16)
    mine = (partial[:, 0] + swap(away, "tp").astype(f32)).astype(bf16)
    back = t_send([mine[1], mine[2], mine[3]])
    total = mine[0].astype(f32)
    for b in back:
        total = total + b.astype(f32)
    return total


def gather_g(value):
    if lax.axis_size("z1") == 2:
        first = jnp.stack([value, swap(value, "z1")])
    else:
        first = lax.all_gather(value, "z1", axis=0)
    return jnp.stack([first, swap(first, "y")], axis=1)


def reduce_g(value):
    half = (value[:, 0] + swap(value[:, 1].astype(bf16), "y").astype(f32))
    if lax.axis_size("z1") == 2:
        return half[0] + swap(half[1].astype(bf16), "z1").astype(f32)
    got = lax.all_to_all(half.astype(bf16), "z1", 0, 0, tiled=True)
    return jnp.sum(got.astype(f32), axis=0)


def relative_order(n1, rows):
    width = n1 * 8 * rows
    place = lax.broadcasted_iota(jnp.int32, (1, width), 1)
    row = place % rows
    rest = place // rows
    x = rest % 2
    z0 = (rest // 2) % 2
    y = ((rest // 4) % 2) ^ lax.axis_index("y")
    z1 = rest // 8
    if n1 == 2:
        z1 = z1 ^ lax.axis_index("z1")
    return (((z1 * 2 + z0) * 2 + y) * 2 + x) * rows + row


def on_device(
    tokens, cotangent, parents, skip, w_query, key_matrix, value_matrix, w_out, w_gate, w_up, w_down, gain_attn, gain_mlp
):
    half_rows, width = tokens.shape
    seq_len = 2 * half_rows
    rows = w_query.shape[0]
    n1 = lax.axis_size("z1")
    q_cols = w_query.shape[1]
    kv_cols = key_matrix.shape[1]
    heads = q_cols // HEAD_SIZE
    kv_heads = kv_cols // HEAD_SIZE
    group = heads // kv_heads
    ff = w_gate.shape[1]
    hs = -(-ff // (4 * LANES)) * LANES
    scale = HEAD_SIZE ** (-0.5)
    core = lax.axis_index("tp")
    active = (1 - skip[0]).astype(f32)
    cos_np, sin_np = rotary_tables(seq_len, heads)
    cosine, sine = jnp.asarray(cos_np), jnp.asarray(sin_np)
    visible = np.tril(np.ones((seq_len, seq_len), bool))

    gain_one = gain_attn.astype(f32)[:, None]
    gain_two = gain_mlp.astype(f32)[:, None]

    scaled_w = lambda w, g: (w.astype(f32) * g).astype(bf16)
    attn_w = jnp.concatenate(
        [scaled_w(w_query, gain_one), scaled_w(key_matrix, gain_one), scaled_w(value_matrix, gain_one), w_out.T], axis=1
    )
    along_z = spread(attn_w, ("z1", "z0"))
    everywhere = spread(along_z, ("y", "x"))
    attn_all = everywhere.transpose(1, 0, 2, 3).reshape(width, attn_w.shape[1])
    qkv_w = attn_all[:, : q_cols + 2 * kv_cols]
    out_t = attn_all[:, q_cols + 2 * kv_cols :]

    pad = lambda w: jnp.pad(w, ((0, 0), (0, 4 * hs - ff))).reshape(rows, 4, hs).transpose(1, 0, 2)
    gate_up = jnp.concatenate([pad(scaled_w(w_gate, gain_two)), pad(scaled_w(w_up, gain_two))], axis=2)
    down = pad(w_down.T)
    gu_t = lax.all_to_all(gate_up, T_AXES, 0, 0, tiled=True).reshape(4 * rows, 2 * hs)
    down_t = lax.all_to_all(down, T_AXES, 0, 0, tiled=True).reshape(4 * rows, hs)
    gu_all = gather_g(gu_t).reshape(width, 2 * hs)
    down_all = gather_g(down_t).reshape(width, hs)
    order = relative_order(n1, rows)
    natural = lax.broadcasted_iota(jnp.int32, (width, 1), 0)
    to_relative = (natural == order).astype(bf16)

    other_tokens, other_cot = swap(tokens, "tp"), swap(cotangent, "tp")
    both = lambda mine, other: jnp.where(core == 0, jnp.stack([mine, other]), jnp.stack([other, mine])).reshape(seq_len, width)
    inputs = both(tokens, other_tokens).astype(f32)
    grad_out = both(cotangent, other_cot).astype(f32)
    my_half = lambda v: lax.dynamic_slice_in_dim(v, core * half_rows, half_rows, axis=0)

    grad_mlp = (active * cotangent.astype(f32)).astype(bf16)
    cot_all = share_tokens(nn(grad_mlp, to_relative).astype(bf16)).reshape(8 * half_rows, width)

    stat_one = lax.rsqrt(jnp.mean(inputs * inputs, axis=-1, keepdims=True) + eps)
    scaled_one = inputs * stat_one
    normed = scaled_one.astype(bf16)
    qkv = nn(normed, qkv_w)
    query = rotate(qkv[:, :q_cols], cosine, sine).astype(bf16)
    key = rotate(qkv[:, q_cols : q_cols + kv_cols], cosine, sine).astype(bf16)
    value = qkv[:, q_cols + kv_cols :].astype(bf16)
    q4 = query.reshape(seq_len, kv_heads, group, HEAD_SIZE)
    k3 = key.reshape(seq_len, kv_heads, HEAD_SIZE)
    v3 = value.reshape(seq_len, kv_heads, HEAD_SIZE)
    raw = jnp.einsum("qhgd,khd->hgqk", q4, k3, preferred_element_type=f32) * scale
    scores = jnp.where(visible, raw, -1e30)
    row_max = jnp.max(scores, axis=-1, keepdims=True)
    exponent = jnp.exp(scores - row_max)
    probs = exponent / jnp.sum(exponent, axis=-1, keepdims=True)
    probs_low = probs.astype(bf16)
    attended = jnp.einsum("hgqk,khd->qhgd", probs_low, v3, preferred_element_type=f32)
    attended = attended.reshape(seq_len, q_cols).astype(bf16)
    branch_part = nt(attended, out_t)
    branch = branch_part + swap(branch_part.astype(bf16), "tp").astype(f32)
    branch = branch_part.astype(bf16).astype(f32) + (branch - branch_part)
    middle = inputs + active * branch
    stat_two = lax.rsqrt(jnp.mean(middle * middle, axis=-1, keepdims=True) + eps)
    scaled_two = middle * stat_two
    x_all = share_tokens(nn(my_half(scaled_two).astype(bf16), to_relative).astype(bf16)).reshape(8 * half_rows, width)

    gu = nn(x_all, gu_all)
    gate, up = gu[:, :hs], gu[:, hs:]
    sig = jax.nn.sigmoid(gate)
    hidden = (gate * sig * up).astype(bf16)
    d_hidden = nt(cot_all, down_all.T) if False else nn(cot_all, down_all)
    d_gate = (d_hidden * up * sig * (1.0 + gate * (1.0 - sig))).astype(bf16)
    d_up = (d_hidden * gate * sig).astype(bf16)
    d_gu = jnp.concatenate([d_gate, d_up], axis=1)
    e_part = nt(d_gu, gu_all).reshape(4, 2, half_rows, width)
    e_rel = return_tokens(e_part).astype(bf16)
    e_mine = nt(e_rel, to_relative).astype(bf16)
    grad_down_rel = tn(cot_all, hidden)
    grad_gu_rel = tn(x_all, d_gu)
    mlp_part = nt(hidden, down_all).reshape(4, 2, half_rows, width)
    mlp_mine = nt(return_tokens(mlp_part).astype(bf16), to_relative)
    output = (my_half(middle) + active * mlp_mine).astype(bf16)

    def to_owner(grad):
        cols = grad.shape[1]
        summed = reduce_g(grad.reshape(n1, 2, 4 * rows, cols)).astype(bf16).reshape(4, rows, cols)
        return lax.all_to_all(summed, T_AXES, 0, 0, tiled=True)

    got_down = to_owner(grad_down_rel)
    got_gu = to_owner(grad_gu_rel)
    join = lambda v: v.transpose(1, 0, 2).reshape(rows, 4 * hs)[:, :ff].astype(f32)
    dg_scaled = join(got_gu[:, :, :hs])
    du_scaled = join(got_gu[:, :, hs:])
    grad_w_gate = dg_scaled * gain_two
    grad_w_up = du_scaled * gain_two
    grad_w_down = join(got_down).T

    e_two = both(e_mine, swap(e_mine, "tp")).astype(f32)
    d_middle = grad_out + stat_two * (e_two - scaled_two * jnp.mean(e_two * scaled_two, axis=-1, keepdims=True))
    d_branch = (active * d_middle).astype(bf16)
    d_attended = nn(d_branch, out_t).astype(bf16)
    da4 = d_attended.reshape(seq_len, kv_heads, group, HEAD_SIZE)
    d_probs = jnp.einsum("qhgd,khd->hgqk", da4, v3, preferred_element_type=f32)
    d_value = jnp.einsum("hgqk,qhgd->khd", probs_low, da4, preferred_element_type=f32).reshape(seq_len, kv_cols).astype(bf16)
    d_scores = (probs * (d_probs - jnp.sum(probs * d_probs, axis=-1, keepdims=True))).astype(bf16)
    d_query = jnp.einsum("hgqk,khd->qhgd", d_scores, k3, preferred_element_type=f32).reshape(seq_len, q_cols) * scale
    d_key = jnp.einsum("hgqk,qhgd->khd", d_scores, q4, preferred_element_type=f32).reshape(seq_len, kv_cols) * scale
    d_query = rotate(d_query, cosine, -sine).astype(bf16)
    d_key = rotate(d_key, cosine, -sine).astype(bf16)
    d_qkv = jnp.concatenate([d_query, d_key, d_value], axis=1)
    attn_grad = jnp.concatenate([tn(normed, d_qkv), tn(d_branch, attended)], axis=1).astype(bf16)
    cols = attn_grad.shape[1]
    blocks = attn_grad.reshape(2 * n1, 4, rows, cols).transpose(1, 0, 2, 3)
    got = lax.all_to_all(blocks, ("y", "x"), 0, 0, tiled=True)
    got = jnp.sum(got.astype(f32), axis=0).astype(bf16)
    got = lax.all_to_all(got, ("z1", "z0"), 0, 0, tiled=True)
    owned = jnp.sum(got.astype(f32), axis=0)
    e_part_one = nt(d_qkv, qkv_w)
    e_away = lax.dynamic_slice_in_dim(e_part_one, (1 - core) * half_rows, half_rows, axis=0).astype(bf16)
    e_one = my_half(e_part_one) + swap(e_away, "tp").astype(f32)
    s_one = my_half(scaled_one)
    grad_tokens = (
        my_half(d_middle) + my_half(stat_one) * (e_one - s_one * jnp.mean(e_one * s_one, axis=-1, keepdims=True))
    ).astype(bf16)

    dq_s = owned[:, :q_cols]
    dk_s = owned[:, q_cols : q_cols + kv_cols]
    dv_s = owned[:, q_cols + kv_cols : q_cols + 2 * kv_cols]
    row_sum = lambda w, d: jnp.sum(w.astype(f32) * d, axis=1)
    gain_parts = jnp.stack(
        [
            row_sum(w_query, dq_s) + row_sum(key_matrix, dk_s) + row_sum(value_matrix, dv_s),
            row_sum(w_gate, dg_scaled) + row_sum(w_up, du_scaled),
        ]
    )
    gains = gain_parts + swap(gain_parts, "tp")
    return (
        output,
        grad_tokens,
        dq_s * gain_one,
        dk_s * gain_one,
        dv_s * gain_one,
        owned[:, q_cols + 2 * kv_cols :].T,
        grad_w_gate,
        grad_w_up,
        grad_w_down,
        gains[0],
        gains[1],
    )


def solution(mesh):
    n1 = mesh.shape["fsdp"] // 8
    fine = Mesh(mesh.devices.reshape(n1, 2, 2, 2, mesh.shape["tp"]), ("z1", "z0", "y", "x", "tp"))
    fs = ("z1", "z0", "y", "x")
    both = fs + ("tp",)
    in_specs = (
        P(both, None), P(both, None), P(fs, None), P(fs),
        P(fs, "tp"), P(fs, "tp"), P(fs, "tp"), P("tp", fs),
        P(fs, "tp"), P(fs, "tp"), P("tp", fs), P(fs), P(fs),
    )
    out_specs = (
        P(both, None), P(both, None), P(fs, "tp"), P(fs, "tp"), P(fs, "tp"), P("tp", fs),
        P(fs, "tp"), P(fs, "tp"), P("tp", fs), P(fs), P(fs),
    )
    return jax.shard_map(on_device, mesh=fine, in_specs=in_specs, out_specs=out_specs, check_vma=False)
```

time: 1260 us -> 288 us (0.23)
  waiting for transfers between devices: 805 us -> 96.4 us
  blocking collectives: 320 us -> 11.1 us
  starting transfers between devices: 4.91 us -> 60.2 us
  local copies, waits for them, and re-layouts: 13.3 us -> 34.7 us
  matrix products: 52.7 us -> 32.9 us
  between operations: 18.2 us -> 2.6 us
    unnamed x9 -> x0, waiting for transfers between devices: 595 us -> none
    all_gather x3 -> x0, waiting for transfers between devices: 210 us -> none  [the longest x1 73.4 us: fetch_mlp(): lax.all_gather(w_gate, 'fsdp', axis=0, tiled=True)]
    all_gather x8 -> x0, blocking collectives: 169 us -> none  [the longest x1 43.4 us: fetch_attention(): lax.all_gather(w_out, 'fsdp', axis=1, tiled=True)]
    psum x1 -> x0, blocking collectives: 107 us -> none  [on_device(): lax.psum((grad_gain_one, grad_gain_two), ('fsdp', 'tp'))]
    ppermute x0 -> x30, waiting for transfers between devices: none -> 52.2 us  [the longest x18 42 us: swap(): return lax.ppermute(value, axis, SWAP)]
    unnamed x1 -> x0, blocking collectives: 44.2 us -> none
    all_to_all x1 -> x7, waiting for transfers between devices: 0.01 us -> 44.2 us  [the longest x2 28.8 us: spread(): return lax.all_to_all(wide, axes, 0, 0, tiled=True)]
    ppermute x0 -> x30, starting transfers between devices: none -> 30.4 us  [the longest x12 17.5 us: t_send(): lax.ppermute(v, T_AXES, t_partner(xb, zb))]
  transfers between devices with their start and end apart: 9 -> 37, of which waited for: 4 -> 12; matrix products, arithmetic and copies ran while one was open for 5% -> 31% of each run, Pallas kernels for 0% -> 0%
where the time goes in v1:
time: 288 us; the launch traced here: 286 us
  waiting for transfers between devices  96.4 us (33%)
  starting transfers between devices  60.2 us (21%)
  other arithmetic  48.4 us (17%)
  local copies, waits for them, and re-layouts  34.7 us (12%)
  matrix products  32.9 us (11%)
  blocking collectives  11.1 us (4%)
    ppermute x18, waiting for transfers between devices, swap(): return lax.ppermute(value, axis, SWAP)  42 us
    all_to_all x2, waiting for transfers between devices, spread(): return lax.all_to_all(wide, axes, 0, 0, tiled=True)  28.8 us
    ppermute x12, starting transfers between devices, t_send(): lax.ppermute(v, T_AXES, t_partner(xb, zb))  17.5 us
    ppermute x18, starting transfers between devices, swap(): return lax.ppermute(value, axis, SWAP)  13 us
    all_to_all x1, blocking collectives, on_device(): lax.all_to_all(gate_up, T_AXES, 0, 0, tiled=True).reshape(4 * rows, 2 * hs)  11.1 us
    all_to_all x1, waiting for transfers between devices, on_device(): got = lax.all_to_all(got, ('z1', 'z0'), 0, 0, tiled=True)  10.7 us
    dot_general x6, matrix products, nt(): lax.dot_general(a, b, (((1,), (1,)), ((), ())), preferred_element_type=f32)  10.6 us
    dot_general x4, local copies, waits for them, and re-layouts, tn(): lax.dot_general(a, b, (((0,), (0,)), ((), ())), preferred_element_type=f32)  10.5 us
  transfers between devices with their start and end apart: 37, of which 12 were waited for; matrix products, arithmetic and copies ran while one was open for 31% of the time, Pallas kernels for 0%

profile of v1, /device:TPU:0, one launch (start us, length us, event | category | flops | bytes accessed | tf_op | source)
XLA Modules:
  0.0 286.3 jit_solution(16040832656170147369)
XLA Ops:
  4.9 6.3 %all-to-all-start = ((bf16[4,56,1024]{2,1,0:T(8,128)(2,1)}), bf16[4,56,1024]{2,1,0:T(8,128)(2,1)S(1)}, u32[]{:S(2)}, u32[]{:S(2)}) async-start(bf16[4,56,1024]{2,1,0:T(8,128)(2,1)} %broadcast_in_dim.16), calls=%async_computation | async-start | bytes 917504 | tf_op jit(solution)/shard_map/all_to_all | solution.py:56
  12.2 12.1 %all-to-all-done = bf16[4,56,1024]{2,1,0:T(8,128)(2,1)S(1)} async-done(((bf16[4,56,1024]{2,1,0:T(8,128)(2,1)}), bf16[4,56,1024]{2,1,0:T(8,128)(2,1)S(1)}, u32[]{:S(2)}, u32[]{:S(2)}) %all-to-all-start) | async-done | bytes 458784 | tf_op jit(solution)/shard_map/all_to_all | solution.py:56
  24.3 11.1 %all_to_all.40 = bf16[4,56,1280]{2,1,0:T(8,128)(2,1)S(1)} all-to-all(bf16[4,56,1280]{2,1,0:T(8,128)(2,1)S(1)} %copy.123), channel_id=1, replica_groups=mesh['z1'=2,'z0'=2,'y'=2,'x'=2,'tp'=2] {'z0','x'}, dimensions={0} | all-to-all | bytes 1146880 | tf_op jit(solution)/shard_map/all_to_all | solution.py:155
  36.9 3.7 %all-to-all-start.1 = ((bf16[4,4,56,1024]{3,2,1,0:T(8,128)(2,1)}), bf16[4,4,56,1024]{3,2,1,0:T(8,128)(2,1)S(1)}, u32[]{:S(2)}, u32[]{:S(2)}) async-start(bf16[4,4,56,1024]{3,2,1,0:T(8,128)(2,1)} %broadcast_in_dim.19), calls=%async_computation.1 | async-start | bytes 3670016 | tf_op jit(solution)/shard_map/all_to_all | solution.py:56
  42.9 2.1 collective-permute-start.17
  48.7 2.0 convert_bitcast_fusion.1
  51.5 16.7 %all-to-all-done.1 = bf16[4,4,56,1024]{3,2,1,0:T(8,128)(2,1)S(1)} async-done(((bf16[4,4,56,1024]{3,2,1,0:T(8,128)(2,1)}), bf16[4,4,56,1024]{3,2,1,0:T(8,128)(2,1)S(1)}, u32[]{:S(2)}, u32[]{:S(2)}) %all-to-all-start.1) | async-done | bytes 1835040 | tf_op jit(solution)/shard_map/all_to_all | solution.py:56
  69.5 4.1 %all-to-all-start.3 = ((bf16[4,56,640]{2,1,0:T(8,128)(2,1)}), bf16[4,56,640]{2,1,0:T(8,128)(2,1)}, u32[]{:S(2)}, u32[]{:S(2)}) async-start(bf16[4,56,640]{2,1,0:T(8,128)(2,1)} %copy.125), calls=%async_computation.3 | async-start | bytes 573440 | tf_op jit(solution)/shard_map/all_to_all | solution.py:156
  79.8 2.9 fusion.126
  83.2 2.6 fusion.125
  87.3 2.0 multiply_reduce_fusion
  90.3 2.9 %collective-permute-start.4 = (bf16[128,896]{1,0:T(8,128)(2,1)S(1)}, bf16[128,896]{1,0:T(8,128)(2,1)S(1)}, u32[]{:S(2)}, u32[]{:S(2)}) collective-permute-start(bf16[128,896]{1,0:T(8,128)(2,1)S(1)} %fusion.26), channel_id=1, source_target_pairs={{0,10},{2,8},{8,2},{10,0},{1,11},{3,9},{9,3},{11,1},{4,14},{6,12},... | collective-permute-start | bytes 688136 | tf_op jit(solution)/shard_map/ppermute | solution.py:67
  93.8 5.4 %collective-permute-done.8 = bf16[224,640]{1,0:T(8,128)(2,1)S(1)} collective-permute-done((bf16[224,640]{1,0:T(8,128)(2,1)}, bf16[224,640]{1,0:T(8,128)(2,1)S(1)}, u32[]{:S(2)}, u32[]{:S(2)}) %collective-permute-start.8) | collective-permute-done | bytes 286752 | tf_op jit(solution)/shard_map/ppermute | solution.py:48
  99.2 2.0 collective-permute-start.2
  101.2 1.9 fusion.124
  103.1 1.8 collective-permute-done.4
  104.9 3.6 %collective-permute-done.3 = bf16[128,896]{1,0:T(8,128)(2,1)S(1)} collective-permute-done((bf16[128,896]{1,0:T(8,128)(2,1)S(1)}, bf16[128,896]{1,0:T(8,128)(2,1)S(1)}, u32[]{:S(2)}, u32[]{:S(2)}) %collective-permute-start.3) | collective-permute-done | bytes 229408 | tf_op jit(solution)/shard_map/ppermute | solution.py:67
  110.5 2.0 copy.135
  113.6 1.9 maximum_select_fusion.1
  118.6 3.8 %copy.142 = bf16[896,1024]{1,0:T(8,128)(2,1)} copy(bf16[896,1024]{0,1:T(8,128)(2,1)} %bitcast.317) | data formatting | bytes 3670016 | tf_op jit(solution)/shard_map/dot_general | solution.py:40
  122.4 3.2 %collective-permute-done.9 = bf16[2,224,640]{2,1,0:T(8,128)(2,1)} collective-permute-done((bf16[2,224,640]{2,1,0:T(8,128)(2,1)}, bf16[2,224,640]{2,1,0:T(8,128)(2,1)}, u32[]{:S(2)}, u32[]{:S(2)}) %collective-permute-start.9) | collective-permute-done | bytes 573472 | tf_op jit(solution)/shard_map/ppermute | solution.py:48
  129.9 2.9 %fusion.134 = f32[1024,1280]{1,0:T(8,128)S(1)} fusion(bf16[1024,896]{1,0:T(8,128)(2,1)S(1)} %bitcast.315, bf16[896,1280]{1,0:T(8,128)(2,1)S(1)} %bitcast.322), kind=kOutput, calls=%fused_computation.261 | convolution fusion | flops 2348810240 | bytes 9371648 | tf_op jit(solution)/shard_map/dot_general | solution.py:36
  132.8 2.4 multiply_convert_fusion.1
  135.3 1.7 fusion.135
  138.1 1.8 copy-done.23
  143.3 2.9 %fusion.136 = f32[4,2,128,896]{3,2,1,0:T(8,128)S(1)} fusion(bf16[4,2,128,1280]{3,2,1,0:T(8,128)(2,1)S(1)} %bitcast.319, bf16[896,1280,1,1]{1,0,3,2:T(8,128)(2,1)S(1)} %bitcast.323), kind=kOutput, calls=%fused_computation.263 | convolution fusion | flops 2348810240 | bytes 8585216 | tf_op jit(solution)/shard_map/dot_general | solution.py:44
  146.2 1.8 copy-done.19
  149.1 3.8 %copy.138 = bf16[896,1024]{1,0:T(8,128)(2,1)} copy(bf16[896,1024]{0,1:T(8,128)(2,1)} %bitcast.316) | data formatting | bytes 3670016 | tf_op jit(solution)/shard_map/dot_general | solution.py:40
  152.9 4.9 %fusion.4 = f32[2,2,224,1280]{3,2,1,0:T(8,128)S(1)} fusion(bf16[2,2,224,1024]{3,2,1,0:T(8,128)(2,1)} %bitcast.331, bf16[1024,640]{1,0:T(8,128)(2,1)} %copy-done.27, bf16[1024,640]{1,0:T(8,128)(2,1)} %copy-done.26), kind=kOutput, calls=%fused_computation.6 | convolution fusion | flops 2354053120 | bytes 9043968 | tf_op jit(solution)/shard_map/dot_general | solution.py:40
  159.5 2.7 collective-permute-start.28
  164.7 11.2 %collective-permute-done.28 = bf16[224,640]{1,0:T(8,128)(2,1)S(1)} collective-permute-done((bf16[224,640]{1,0:T(8,128)(2,1)S(1)}, bf16[224,640]{1,0:T(8,128)(2,1)S(1)}, u32[]{:S(2)}, u32[]{:S(2)}) %collective-permute-start.28) | collective-permute-done | bytes 286752 | tf_op jit(solution)/shard_map/ppermute | solution.py:48
  176.6 3.5 %all-to-all-start.7 = ((bf16[4,56,640]{2,1,0:T(8,128)(2,1)}), bf16[4,56,640]{2,1,0:T(8,128)(2,1)S(1)}, u32[]{:S(2)}, u32[]{:S(2)}) async-start(bf16[4,56,640]{2,1,0:T(8,128)(2,1)} %bitcast.131), calls=%async_computation.7 | async-start | bytes 573440 | tf_op jit(solution)/shard_map/all_to_all | solution.py:218
  180.1 2.1 fusion.8
  182.3 2.9 %collective-permute-start.22 = (bf16[128,896]{1,0:T(8,128)(2,1)S(1)}, bf16[128,896]{1,0:T(8,128)(2,1)S(1)}, u32[]{:S(2)}, u32[]{:S(2)}) collective-permute-start(bf16[128,896]{1,0:T(8,128)(2,1)S(1)} %get-tuple-element.23), channel_id=1, source_target_pairs={{0,10},{2,8},{8,2},{10,0},{1,11},{3,9},{9,3},{11,1},{4,14},{6,12},... | collective-permute-start | bytes 688136 | tf_op jit(solution)/shard_map/ppermute | solution.py:67
  188.3 2.8 collective-permute-start.13
  193.8 3.4 %collective-permute-done.21 = bf16[128,896]{1,0:T(8,128)(2,1)S(1)} collective-permute-done((bf16[128,896]{1,0:T(8,128)(2,1)S(1)}, bf16[128,896]{1,0:T(8,128)(2,1)S(1)}, u32[]{:S(2)}, u32[]{:S(2)}) %collective-permute-start.21) | collective-permute-done | bytes 229408 | tf_op jit(solution)/shard_map/ppermute | solution.py:67
  199.1 3.0 %fusion.6 = f32[2,224,1280]{2,1,0:T(8,128)} fusion(f32[2,2,224,1280]{3,2,1,0:T(8,128)S(1)} %copy-done.15, bf16[2,224,1280]{2,1,0:T(8,128)(2,1)} %collective-permute-done.25), kind=kLoop, calls=%fused_computation.14 | loop fusion | flops 1146880 | bytes 5734400 | tf_op jit(solution)/shard_map/add | solution.py:97
  215.4 4.4 %all-to-all-start.4 = ((bf16[4,4,56,1024]{3,2,1,0:T(8,128)(2,1)}), bf16[4,4,56,1024]{3,2,1,0:T(8,128)(2,1)}, u32[]{:S(2)}, u32[]{:S(2)}) async-start(bf16[4,4,56,1024]{3,2,1,0:T(8,128)(2,1)} %copy.137), calls=%async_computation.4 | async-start | bytes 3670016 | tf_op jit(solution)/shard_map/all_to_all | solution.py:245
  221.1 3.5 %collective-permute-start.26 = (bf16[224,1280]{1,0:T(8,128)(2,1)S(1)}, bf16[224,1280]{1,0:T(8,128)(2,1)S(1)}, u32[]{:S(2)}, u32[]{:S(2)}) collective-permute-start(bf16[224,1280]{1,0:T(8,128)(2,1)S(1)} %fusion.56), channel_id=1, source_target_pairs={{0,16},{16,0},{1,17},{17,1},{2,18},{18,2},{3,19},{19,3},{4,20},{20... | collective-permute-start | bytes 1720328 | tf_op jit(solution)/shard_map/ppermute | solution.py:48
  224.6 2.8 fusion.25
  228.4 22.1 %collective-permute-done.26 = bf16[224,1280]{1,0:T(8,128)(2,1)S(1)} collective-permute-done((bf16[224,1280]{1,0:T(8,128)(2,1)S(1)}, bf16[224,1280]{1,0:T(8,128)(2,1)S(1)}, u32[]{:S(2)}, u32[]{:S(2)}) %collective-permute-start.26) | collective-permute-done | bytes 573472 | tf_op jit(solution)/shard_map/ppermute | solution.py:48
  251.4 3.5 %all-to-all-start.6 = ((bf16[4,56,1280]{2,1,0:T(8,128)(2,1)}), bf16[4,56,1280]{2,1,0:T(8,128)(2,1)S(1)}, u32[]{:S(2)}, u32[]{:S(2)}) async-start(bf16[4,56,1280]{2,1,0:T(8,128)(2,1)} %bitcast.120), calls=%async_computation.6 | async-start | bytes 1146880 | tf_op jit(solution)/shard_map/all_to_all | solution.py:218
  256.4 2.7 reduce_sum.126
  259.1 4.6 %all-to-all-done.6 = bf16[4,56,1280]{2,1,0:T(8,128)(2,1)S(1)} async-done(((bf16[4,56,1280]{2,1,0:T(8,128)(2,1)}), bf16[4,56,1280]{2,1,0:T(8,128)(2,1)S(1)}, u32[]{:S(2)}, u32[]{:S(2)}) %all-to-all-start.6) | async-done | bytes 573472 | tf_op jit(solution)/shard_map/all_to_all | solution.py:218
  263.7 4.4 %all-to-all-start.5 = ((bf16[4,56,1024]{2,1,0:T(8,128)(2,1)}), bf16[4,56,1024]{2,1,0:T(8,128)(2,1)S(1)}, u32[]{:S(2)}, u32[]{:S(2)}) async-start(bf16[4,56,1024]{2,1,0:T(8,128)(2,1)} %reduce_sum.126), calls=%async_computation.5 | async-start | bytes 917504 | tf_op jit(solution)/shard_map/all_to_all | solution.py:247
  268.3 2.3 fusion.62
  270.6 10.7 %all-to-all-done.5 = bf16[4,56,1024]{2,1,0:T(8,128)(2,1)S(1)} async-done(((bf16[4,56,1024]{2,1,0:T(8,128)(2,1)}), bf16[4,56,1024]{2,1,0:T(8,128)(2,1)S(1)}, u32[]{:S(2)}, u32[]{:S(2)}) %all-to-all-start.5) | async-done | bytes 458784 | tf_op jit(solution)/shard_map/all_to_all | solution.py:247
  284.0 1.8 add_convert_fusion
  (293 shorter events, 72.9 us)
Async XLA Ops:
  4.9 19.4 %all-to-all-start = ((bf16[4,56,1024]{2,1,0:T(8,128)(2,1)}), bf16[4,56,1024]{2,1,0:T(8,128)(2,1)S(1)}, u32[]{:S(2)}, u32[]{:S(2)}) async-start(bf16[4,56,1024]{2,1,0:T(8,128)(2,1)} %broadcast_in_dim.16), calls=%async_computation | async-start | bytes 917504 | tf_op jit(solution)/shard_map/all_to_all | solution.py:56
  36.9 31.4 %all-to-all-start.1 = ((bf16[4,4,56,1024]{3,2,1,0:T(8,128)(2,1)}), bf16[4,4,56,1024]{3,2,1,0:T(8,128)(2,1)S(1)}, u32[]{:S(2)}, u32[]{:S(2)}) async-start(bf16[4,4,56,1024]{3,2,1,0:T(8,128)(2,1)} %broadcast_in_dim.19), calls=%async_computation.1 | async-start | bytes 3670016 | tf_op jit(solution)/shard_map/all_to_all | solution.py:56
  40.6 7.3 %collective-permute-start = (bf16[128,896]{1,0:T(8,128)(2,1)S(1)}, bf16[128,896]{1,0:T(8,128)(2,1)S(1)}, u32[]{:S(2)}, u32[]{:S(2)}) collective-permute-start(bf16[128,896]{1,0:T(8,128)(2,1)S(1)} %copy-done.20), channel_id=1, source_target_pairs={{0,1},{1,0},{2,3},{3,2},{4,5},{5,4},{6,7},{7,6},{8,9},{9,8},{10,11... | collective-permute-start | bytes 688136 | tf_op jit(solution)/shard_map/ppermute | solution.py:48
  42.9 36.9 %collective-permute-start.17 = (bf16[128,896]{1,0:T(8,128)(2,1)}, bf16[128,896]{1,0:T(8,128)(2,1)}, u32[]{:S(2)}, u32[]{:S(2)}) collective-permute-start(bf16[128,896]{1,0:T(8,128)(2,1)} %fusion.27), channel_id=1, source_target_pairs={{0,10},{2,8},{8,2},{10,0},{1,11},{3,9},{9,3},{11,1},{4,14},{6,12},... | collective-permute-start | bytes 688136 | tf_op jit(solution)/shard_map/ppermute | solution.py:67
  45.0 34.8 %collective-permute-start.16 = (bf16[128,896]{1,0:T(8,128)(2,1)}, bf16[128,896]{1,0:T(8,128)(2,1)}, u32[]{:S(2)}, u32[]{:S(2)}) collective-permute-start(bf16[128,896]{1,0:T(8,128)(2,1)} %fusion.27), channel_id=1, source_target_pairs={{0,8},{2,10},{8,0},{10,2},{1,9},{3,11},{9,1},{11,3},{4,12},{6,14},... | collective-permute-start | bytes 688136 | tf_op jit(solution)/shard_map/ppermute | solution.py:67
  46.3 33.5 %collective-permute-start.15 = (bf16[128,896]{1,0:T(8,128)(2,1)}, bf16[128,896]{1,0:T(8,128)(2,1)}, u32[]{:S(2)}, u32[]{:S(2)}) collective-permute-start(bf16[128,896]{1,0:T(8,128)(2,1)} %fusion.27), channel_id=1, source_target_pairs={{0,2},{2,0},{8,10},{10,8},{1,3},{3,1},{9,11},{11,9},{4,6},{6,4},{1... | collective-permute-start | bytes 688136 | tf_op jit(solution)/shard_map/ppermute | solution.py:67
  50.7 24.6 %copy-start = (f32[256,896]{1,0:T(8,128)}, f32[256,896]{1,0:T(8,128)S(1)}, u32[]{:S(2)}) copy-start(f32[256,896]{1,0:T(8,128)S(1)} %get-tuple-element.41) | copy-start | bytes 2752516
  50.7 32.5 %collective-permute-start.6 = (bf16[224,1280]{1,0:T(8,128)(2,1)S(1)}, bf16[224,1280]{1,0:T(8,128)(2,1)}, u32[]{:S(2)}, u32[]{:S(2)}) collective-permute-start(bf16[224,1280]{1,0:T(8,128)(2,1)S(1)} %bitcast.320), channel_id=1, source_target_pairs={{0,16},{16,0},{1,17},{17,1},{2,18},{18,2},{3,19},{19,3},{4,20},{20... | collective-permute-start | bytes 1720328 | tf_op jit(solution)/shard_map/ppermute | solution.py:48
  69.5 13.5 %all-to-all-start.3 = ((bf16[4,56,640]{2,1,0:T(8,128)(2,1)}), bf16[4,56,640]{2,1,0:T(8,128)(2,1)}, u32[]{:S(2)}, u32[]{:S(2)}) async-start(bf16[4,56,640]{2,1,0:T(8,128)(2,1)} %copy.125), calls=%async_computation.3 | async-start | bytes 573440 | tf_op jit(solution)/shard_map/all_to_all | solution.py:156
  79.8 7.6 %collective-permute-start.1 = (bf16[256,896]{1,0:T(8,128)(2,1)S(1)}, bf16[256,896]{1,0:T(8,128)(2,1)}, u32[]{:S(2)}, u32[]{:S(2)}) collective-permute-start(bf16[256,896]{1,0:T(8,128)(2,1)S(1)} %get-tuple-element.67), channel_id=1, source_target_pairs={{0,1},{1,0},{2,3},{3,2},{4,5},{5,4},{6,7},{7,6},{8,9},{9,8},{10,11... | collective-permute-start | bytes 1376264 | tf_op jit(solution)/shard_map/ppermute | solution.py:48
  82.6 32.9 %collective-permute-start.18 = (bf16[4,128,896]{2,1,0:T(8,128)(2,1)}, bf16[4,128,896]{2,1,0:T(8,128)(2,1)}, u32[]{:S(2)}, u32[]{:S(2)}) collective-permute-start(bf16[4,128,896]{2,1,0:T(8,128)(2,1)} %get-tuple-element.26), channel_id=1, source_target_pairs={{0,1},{1,0},{2,3},{3,2},{4,5},{5,4},{6,7},{7,6},{8,9},{9,8},{10,11... | collective-permute-start | bytes 2752520 | tf_op jit(solution)/shard_map/ppermute | solution.py:48
  83.0 16.2 %collective-permute-start.8 = (bf16[224,640]{1,0:T(8,128)(2,1)}, bf16[224,640]{1,0:T(8,128)(2,1)S(1)}, u32[]{:S(2)}, u32[]{:S(2)}) collective-permute-start(bf16[224,640]{1,0:T(8,128)(2,1)} %bitcast.41), channel_id=1, source_target_pairs={{0,16},{16,0},{1,17},{17,1},{2,18},{18,2},{3,19},{19,3},{4,20},{20... | collective-permute-start | bytes 860168 | tf_op jit(solution)/shard_map/ppermute | solution.py:48
  85.9 40.9 %collective-permute-start.7 = (bf16[2,224,1280]{2,1,0:T(8,128)(2,1)}, bf16[2,224,1280]{2,1,0:T(8,128)(2,1)}, u32[]{:S(2)}, u32[]{:S(2)}) collective-permute-start(bf16[2,224,1280]{2,1,0:T(8,128)(2,1)} %get-tuple-element.21), channel_id=1, source_target_pairs={{0,4},{4,0},{1,5},{5,1},{2,6},{6,2},{3,7},{7,3},{8,12},{12,8},{9,1... | collective-permute-start | bytes 3440648 | tf_op jit(solution)/shard_map/ppermute | solution.py:48
  89.4 13.8 %copy-start.65 = (f32[256]{0:T(256)}, f32[256]{0:T(256)S(1)}, u32[]{:S(2)}) copy-start(f32[256]{0:T(256)S(1)} %add_rsqrt_fusion) | copy-start | bytes 3076
  89.5 15.4 %copy-start.43 = (bf16[128,896]{1,0:T(8,128)(2,1)S(1)}, bf16[128,896]{1,0:T(8,128)(2,1)}, u32[]{:S(2)}) copy-start(bf16[128,896]{1,0:T(8,128)(2,1)} %param.17) | copy-start | bytes 688132
  90.3 14.6 %collective-permute-start.4 = (bf16[128,896]{1,0:T(8,128)(2,1)S(1)}, bf16[128,896]{1,0:T(8,128)(2,1)S(1)}, u32[]{:S(2)}, u32[]{:S(2)}) collective-permute-start(bf16[128,896]{1,0:T(8,128)(2,1)S(1)} %fusion.26), channel_id=1, source_target_pairs={{0,10},{2,8},{8,2},{10,0},{1,11},{3,9},{9,3},{11,1},{4,14},{6,12},... | collective-permute-start | bytes 688136 | tf_op jit(solution)/shard_map/ppermute | solution.py:67
  93.2 15.2 %collective-permute-start.3 = (bf16[128,896]{1,0:T(8,128)(2,1)S(1)}, bf16[128,896]{1,0:T(8,128)(2,1)S(1)}, u32[]{:S(2)}, u32[]{:S(2)}) collective-permute-start(bf16[128,896]{1,0:T(8,128)(2,1)S(1)} %fusion.26), channel_id=1, source_target_pairs={{0,8},{2,10},{8,0},{10,2},{1,9},{3,11},{9,1},{11,3},{4,12},{6,14},... | collective-permute-start | bytes 688136 | tf_op jit(solution)/shard_map/ppermute | solution.py:67
  99.2 9.8 %collective-permute-start.2 = (bf16[128,896]{1,0:T(8,128)(2,1)S(1)}, bf16[128,896]{1,0:T(8,128)(2,1)S(1)}, u32[]{:S(2)}, u32[]{:S(2)}) collective-permute-start(bf16[128,896]{1,0:T(8,128)(2,1)S(1)} %fusion.26), channel_id=1, source_target_pairs={{0,2},{2,0},{8,10},{10,8},{1,3},{3,1},{9,11},{11,9},{4,6},{6,4},{1... | collective-permute-start | bytes 688136 | tf_op jit(solution)/shard_map/ppermute | solution.py:67
  104.9 8.7 %collective-permute-start.14 = (bf16[128,896]{1,0:T(8,128)(2,1)S(1)}, bf16[128,896]{1,0:T(8,128)(2,1)}, u32[]{:S(2)}, u32[]{:S(2)}) collective-permute-start(bf16[128,896]{1,0:T(8,128)(2,1)S(1)} %copy-done.43), channel_id=1, source_target_pairs={{0,1},{1,0},{2,3},{3,2},{4,5},{5,4},{6,7},{7,6},{8,9},{9,8},{10,11... | collective-permute-start | bytes 688136 | tf_op jit(solution)/shard_map/ppermute | solution.py:48
  108.5 17.1 %collective-permute-start.9 = (bf16[2,224,640]{2,1,0:T(8,128)(2,1)}, bf16[2,224,640]{2,1,0:T(8,128)(2,1)}, u32[]{:S(2)}, u32[]{:S(2)}) collective-permute-start(bf16[2,224,640]{2,1,0:T(8,128)(2,1)} %get-tuple-element.35), channel_id=1, source_target_pairs={{0,4},{4,0},{1,5},{5,1},{2,6},{6,2},{3,7},{7,3},{8,12},{12,8},{9,1... | collective-permute-start | bytes 1720328 | tf_op jit(solution)/shard_map/ppermute | solution.py:48
  110.5 17.8 %collective-permute-start.5 = (bf16[4,128,896]{2,1,0:T(8,128)(2,1)}, bf16[4,128,896]{2,1,0:T(8,128)(2,1)}, u32[]{:S(2)}, u32[]{:S(2)}) collective-permute-start(bf16[4,128,896]{2,1,0:T(8,128)(2,1)} %get-tuple-element.31), channel_id=1, source_target_pairs={{0,1},{1,0},{2,3},{3,2},{4,5},{5,4},{6,7},{7,6},{8,9},{9,8},{10,11... | collective-permute-start | bytes 2752520 | tf_op jit(solution)/shard_map/ppermute | solution.py:48
  138.1 47.7 %collective-permute-start.10 = (bf16[4,128,896]{2,1,0:T(8,128)(2,1)}, bf16[4,128,896]{2,1,0:T(8,128)(2,1)}, u32[]{:S(2)}, u32[]{:S(2)}) collective-permute-start(bf16[4,128,896]{2,1,0:T(8,128)(2,1)} %fusion.48), channel_id=1, source_target_pairs={{0,1},{1,0},{2,3},{3,2},{4,5},{5,4},{6,7},{7,6},{8,9},{9,8},{10,11... | collective-permute-start | bytes 2752520 | tf_op jit(solution)/shard_map/ppermute | solution.py:48
  141.6 16.2 %collective-permute-start.27 = (bf16[2,224,640]{2,1,0:T(8,128)(2,1)S(1)}, bf16[2,224,640]{2,1,0:T(8,128)(2,1)}, u32[]{:S(2)}, u32[]{:S(2)}) collective-permute-start(bf16[2,224,640]{2,1,0:T(8,128)(2,1)S(1)} %fusion.57), channel_id=1, source_target_pairs={{0,4},{4,0},{1,5},{5,1},{2,6},{6,2},{3,7},{7,3},{8,12},{12,8},{9,1... | collective-permute-start | bytes 1720328 | tf_op jit(solution)/shard_map/ppermute | solution.py:48
  149.1 31.1 %collective-permute-start.19 = (bf16[4,128,896]{2,1,0:T(8,128)(2,1)}, bf16[4,128,896]{2,1,0:T(8,128)(2,1)}, u32[]{:S(2)}, u32[]{:S(2)}) collective-permute-start(bf16[4,128,896]{2,1,0:T(8,128)(2,1)} %fusion.49), channel_id=1, source_target_pairs={{0,1},{1,0},{2,3},{3,2},{4,5},{5,4},{6,7},{7,6},{8,9},{9,8},{10,11... | collective-permute-start | bytes 2752520 | tf_op jit(solution)/shard_map/ppermute | solution.py:48
  159.5 16.4 %collective-permute-start.28 = (bf16[224,640]{1,0:T(8,128)(2,1)S(1)}, bf16[224,640]{1,0:T(8,128)(2,1)S(1)}, u32[]{:S(2)}, u32[]{:S(2)}) collective-permute-start(bf16[224,640]{1,0:T(8,128)(2,1)S(1)} %fusion.73), channel_id=1, source_target_pairs={{0,16},{16,0},{1,17},{17,1},{2,18},{18,2},{3,19},{19,3},{4,20},{20... | collective-permute-start | bytes 860168 | tf_op jit(solution)/shard_map/ppermute | solution.py:48
  163.3 35.7 %collective-permute-start.25 = (bf16[2,224,1280]{2,1,0:T(8,128)(2,1)}, bf16[2,224,1280]{2,1,0:T(8,128)(2,1)}, u32[]{:S(2)}, u32[]{:S(2)}) collective-permute-start(bf16[2,224,1280]{2,1,0:T(8,128)(2,1)} %fusion.29), channel_id=1, source_target_pairs={{0,4},{4,0},{1,5},{5,1},{2,6},{6,2},{3,7},{7,3},{8,12},{12,8},{9,1... | collective-permute-start | bytes 3440648 | tf_op jit(solution)/shard_map/ppermute | solution.py:48
  176.6 38.7 %all-to-all-start.7 = ((bf16[4,56,640]{2,1,0:T(8,128)(2,1)}), bf16[4,56,640]{2,1,0:T(8,128)(2,1)S(1)}, u32[]{:S(2)}, u32[]{:S(2)}) async-start(bf16[4,56,640]{2,1,0:T(8,128)(2,1)} %bitcast.131), calls=%async_computation.7 | async-start | bytes 573440 | tf_op jit(solution)/shard_map/all_to_all | solution.py:218
  182.3 10.3 %collective-permute-start.22 = (bf16[128,896]{1,0:T(8,128)(2,1)S(1)}, bf16[128,896]{1,0:T(8,128)(2,1)S(1)}, u32[]{:S(2)}, u32[]{:S(2)}) collective-permute-start(bf16[128,896]{1,0:T(8,128)(2,1)S(1)} %get-tuple-element.23), channel_id=1, source_target_pairs={{0,10},{2,8},{8,2},{10,0},{1,11},{3,9},{9,3},{11,1},{4,14},{6,12},... | collective-permute-start | bytes 688136 | tf_op jit(solution)/shard_map/ppermute | solution.py:67
  185.2 12.0 %collective-permute-start.21 = (bf16[128,896]{1,0:T(8,128)(2,1)S(1)}, bf16[128,896]{1,0:T(8,128)(2,1)S(1)}, u32[]{:S(2)}, u32[]{:S(2)}) collective-permute-start(bf16[128,896]{1,0:T(8,128)(2,1)S(1)} %get-tuple-element.24), channel_id=1, source_target_pairs={{0,8},{2,10},{8,0},{10,2},{1,9},{3,11},{9,1},{11,3},{4,12},{6,14},... | collective-permute-start | bytes 688136 | tf_op jit(solution)/shard_map/ppermute | solution.py:67
  185.8 12.3 %copy-start.71 = (s32[896]{0:T(1024)S(1)}, s32[896]{0:T(1024)}, u32[]{:S(2)}) copy-start(s32[896]{0:T(1024)} %copy-done.69) | copy-start | bytes 10756
  185.8 12.3 %collective-permute-start.20 = (bf16[128,896]{1,0:T(8,128)(2,1)S(1)}, bf16[128,896]{1,0:T(8,128)(2,1)S(1)}, u32[]{:S(2)}, u32[]{:S(2)}) collective-permute-start(bf16[128,896]{1,0:T(8,128)(2,1)S(1)} %get-tuple-element.22), channel_id=1, source_target_pairs={{0,2},{2,0},{8,10},{10,8},{1,3},{3,1},{9,11},{11,9},{4,6},{6,4},{1... | collective-permute-start | bytes 688136 | tf_op jit(solution)/shard_map/ppermute | solution.py:67
  185.9 13.2 %copy-start.15 = (f32[2,2,224,1280]{3,2,1,0:T(8,128)S(1)}, f32[2,2,224,1280]{3,2,1,0:T(8,128)}, u32[]{:S(2)}) copy-start(f32[2,2,224,1280]{3,2,1,0:T(8,128)} %copy-done.14) | copy-start | bytes 13762564
  188.3 36.3 %collective-permute-start.13 = (bf16[128,896]{1,0:T(8,128)(2,1)}, bf16[128,896]{1,0:T(8,128)(2,1)}, u32[]{:S(2)}, u32[]{:S(2)}) collective-permute-start(bf16[128,896]{1,0:T(8,128)(2,1)} %get-tuple-element.28), channel_id=1, source_target_pairs={{0,10},{2,8},{8,2},{10,0},{1,11},{3,9},{9,3},{11,1},{4,14},{6,12},... | collective-permute-start | bytes 688136 | tf_op jit(solution)/shard_map/ppermute | solution.py:67
  192.6 32.0 %collective-permute-start.12 = (bf16[128,896]{1,0:T(8,128)(2,1)}, bf16[128,896]{1,0:T(8,128)(2,1)}, u32[]{:S(2)}, u32[]{:S(2)}) collective-permute-start(bf16[128,896]{1,0:T(8,128)(2,1)} %get-tuple-element.29), channel_id=1, source_target_pairs={{0,8},{2,10},{8,0},{10,2},{1,9},{3,11},{9,1},{11,3},{4,12},{6,14},... | collective-permute-start | bytes 688136 | tf_op jit(solution)/shard_map/ppermute | solution.py:67
  197.2 27.4 %collective-permute-start.11 = (bf16[128,896]{1,0:T(8,128)(2,1)}, bf16[128,896]{1,0:T(8,128)(2,1)}, u32[]{:S(2)}, u32[]{:S(2)}) collective-permute-start(bf16[128,896]{1,0:T(8,128)(2,1)} %get-tuple-element.27), channel_id=1, source_target_pairs={{0,2},{2,0},{8,10},{10,8},{1,3},{3,1},{9,11},{11,9},{4,6},{6,4},{1... | collective-permute-start | bytes 688136 | tf_op jit(solution)/shard_map/ppermute | solution.py:67
  199.0 3.1 %collective-permute-start.23 = (bf16[128,896]{1,0:T(8,128)(2,1)S(1)}, bf16[128,896]{1,0:T(8,128)(2,1)S(1)}, u32[]{:S(2)}, u32[]{:S(2)}) collective-permute-start(bf16[128,896]{1,0:T(8,128)(2,1)S(1)} %fusion.28), channel_id=1, source_target_pairs={{0,1},{1,0},{2,3},{3,2},{4,5},{5,4},{6,7},{7,6},{8,9},{9,8},{10,11... | collective-permute-start | bytes 688136 | tf_op jit(solution)/shard_map/ppermute | solution.py:48
  215.4 36.0 %all-to-all-start.4 = ((bf16[4,4,56,1024]{3,2,1,0:T(8,128)(2,1)}), bf16[4,4,56,1024]{3,2,1,0:T(8,128)(2,1)}, u32[]{:S(2)}, u32[]{:S(2)}) async-start(bf16[4,4,56,1024]{3,2,1,0:T(8,128)(2,1)} %copy.137), calls=%async_computation.4 | async-start | bytes 3670016 | tf_op jit(solution)/shard_map/all_to_all | solution.py:245
  221.1 29.4 %collective-permute-start.26 = (bf16[224,1280]{1,0:T(8,128)(2,1)S(1)}, bf16[224,1280]{1,0:T(8,128)(2,1)S(1)}, u32[]{:S(2)}, u32[]{:S(2)}) collective-permute-start(bf16[224,1280]{1,0:T(8,128)(2,1)S(1)} %fusion.56), channel_id=1, source_target_pairs={{0,16},{16,0},{1,17},{17,1},{2,18},{18,2},{3,19},{19,3},{4,20},{20... | collective-permute-start | bytes 1720328 | tf_op jit(solution)/shard_map/ppermute | solution.py:48
  227.4 23.1 %copy-start.7 = (f32[2,224,1280]{2,1,0:T(8,128)S(1)}, f32[2,224,1280]{2,1,0:T(8,128)}, u32[]{:S(2)}) copy-start(f32[2,224,1280]{2,1,0:T(8,128)} %fusion.6) | copy-start | bytes 6881284
  228.1 27.6 %copy-start.1 = (f32[256,896]{1,0:T(8,128)S(1)}, f32[256,896]{1,0:T(8,128)}, u32[]{:S(2)}) copy-start(f32[256,896]{1,0:T(8,128)} %copy-done) | copy-start | bytes 2752516
  228.1 27.6 %collective-permute-start.24 = (bf16[128,896]{1,0:T(8,128)(2,1)S(1)}, bf16[128,896]{1,0:T(8,128)(2,1)S(1)}, u32[]{:S(2)}, u32[]{:S(2)}) collective-permute-start(bf16[128,896]{1,0:T(8,128)(2,1)S(1)} %dynamic-slice_convert_fusion), channel_id=1, source_target_pairs={{0,1},{1,0},{2,3},{3,2},{4,5},{5,4},{6,7},{7,6},{8,9},{9,8},{10,11... | collective-permute-start | bytes 688136 | tf_op jit(solution)/shard_map/ppermute | solution.py:48
  251.4 12.3 %all-to-all-start.6 = ((bf16[4,56,1280]{2,1,0:T(8,128)(2,1)}), bf16[4,56,1280]{2,1,0:T(8,128)(2,1)S(1)}, u32[]{:S(2)}, u32[]{:S(2)}) async-start(bf16[4,56,1280]{2,1,0:T(8,128)(2,1)} %bitcast.120), calls=%async_computation.6 | async-start | bytes 1146880 | tf_op jit(solution)/shard_map/all_to_all | solution.py:218
  263.7 17.6 %all-to-all-start.5 = ((bf16[4,56,1024]{2,1,0:T(8,128)(2,1)}), bf16[4,56,1024]{2,1,0:T(8,128)(2,1)S(1)}, u32[]{:S(2)}, u32[]{:S(2)}) async-start(bf16[4,56,1024]{2,1,0:T(8,128)(2,1)} %reduce_sum.126), calls=%async_computation.5 | async-start | bytes 917504 | tf_op jit(solution)/shard_map/all_to_all | solution.py:247
  268.2 13.3 %copy-start.44 = (bf16[56,448]{1,0:T(8,128)(2,1)S(1)}, bf16[56,448]{1,0:T(8,128)(2,1)}, u32[]{:S(2)}) copy-start(bf16[56,448]{1,0:T(8,128)(2,1)} %param.19) | copy-start | bytes 150532
  268.2 13.3 %copy-start.68 = (f32[56]{0:T(128)S(1)}, f32[56]{0:T(128)}, u32[]{:S(2)}) copy-start(f32[56]{0:T(128)} %copy-done.67) | copy-start | bytes 676
  268.3 15.7 %copy-start.9 = (f32[256,896]{1,0:T(8,128)S(1)}, f32[256,896]{1,0:T(8,128)}, u32[]{:S(2)}) copy-start(f32[256,896]{1,0:T(8,128)} %copy-done.8) | copy-start | bytes 2752516
  268.3 15.7 %copy-start.74 = (f32[128]{0:T(128)S(1)}, f32[128]{0:T(128)}, u32[]{:S(2)}) copy-start(f32[128]{0:T(128)} %fusion.116) | copy-start | bytes 1540
  283.9 1.9 collective-permute-start.29
  (65 other events, 223.0 us)

commit v2 on v1

v2 whole, which is shorter than its diff:
```python
import jax
import jax.numpy as jnp
import numpy as np
from jax import lax
from jax.experimental import pallas as pl
from jax.experimental.pallas import tpu as pltpu
from jax.sharding import Mesh, PartitionSpec as P

HEAD_SIZE = 64
LANES = 128
eps = 1e-05
rotary_base = 10000.0
bf16 = jnp.bfloat16
f32 = jnp.float32
T_AXES = ("z0", "x")
SWAP = [(0, 1), (1, 0)]


def nn(a, b):
    return lax.dot_general(a, b, (((1,), (0,)), ((), ())), preferred_element_type=f32)


def tn(a, b):
    return lax.dot_general(a, b, (((0,), (0,)), ((), ())), preferred_element_type=f32)


def nt(a, b):
    return lax.dot_general(a, b, (((1,), (1,)), ((), ())), preferred_element_type=f32)


def swap(value, axis):
    return lax.ppermute(value, axis, SWAP)


def after(value, *before):
    leaves, tree = jax.tree.flatten(value)
    return jax.tree.unflatten(tree, lax.optimization_barrier(tuple(leaves) + tuple(jax.tree.leaves(before)))[: len(leaves)])


def exchange(blocks, axes):
    return lax.all_to_all(blocks, axes, 0, 0, tiled=True)


def others(value, axes):
    return [lax.ppermute(value, axes, [(i, i ^ k) for i in range(4)]) for k in (1, 2, 3)]


def shape(*dims, dtype=bf16):
    return jax.ShapeDtypeStruct(dims, dtype)


def kernel(body, outs, *args, scalars=None, scratch=()):
    whole = pl.BlockSpec(memory_space=pltpu.VMEM)
    specs = [whole] * len(args)
    if scalars is not None:
        specs = [pl.BlockSpec(memory_space=pltpu.SMEM)] + specs
        args = (scalars,) + args
    return pl.pallas_call(
        body,
        out_shape=list(outs),
        in_specs=specs,
        out_specs=[whole] * len(outs),
        scratch_shapes=list(scratch),
        cost_estimate=pl.CostEstimate(flops=1000, bytes_accessed=1000, transcendentals=0),
        compiler_params=pltpu.CompilerParams(vmem_limit_bytes=60 * 1024 * 1024),
    )(*args)


def join(pieces):
    def body(*refs):
        fill(refs[-1], refs[:-1])

    rows = sum(p.shape[0] for p in pieces)
    return kernel(body, [shape(rows, pieces[0].shape[1])], *pieces)[0]


def gather_line(value):
    if lax.axis_size("z1") == 2:
        return join([value] + others(value, ("z1", "z0")))
    pair = jnp.stack([value, swap(value, "z0")])
    return lax.all_gather(pair, "z1", axis=0).reshape(-1, value.shape[1])


def reduce_y(own, other):
    return (own.astype(f32) + swap(other, "y").astype(f32)).astype(bf16)


def natural_of(n1, rows, letters, relative):
    width = n1 * 8 * rows
    place = lax.broadcasted_iota(jnp.int32, (1, width), 1)
    bits = {}
    rest = place // rows
    for letter in reversed(letters):
        size = n1 if letter == "z1" else 2
        bits[letter] = rest % size
        rest = rest // size
    for letter in letters:
        if letter in relative and (letter != "z1" or n1 == 2):
            bits[letter] = bits[letter] ^ lax.axis_index(letter)
    return (((bits["z1"] * 2 + bits["z0"]) * 2 + bits["y"]) * 2 + bits["x"]) * rows + place % rows


def fill(ref, pieces):
    at = 0
    for p in pieces:
        flat = p[...].reshape(-1, p.shape[-1])
        ref[at : at + flat.shape[0], :] = flat
        at += flat.shape[0]


def column_of(row):
    n = row.shape[1]
    same = lax.broadcasted_iota(jnp.int32, (n, n), 0) == lax.broadcasted_iota(jnp.int32, (n, n), 1)
    return jnp.sum(jnp.where(same, row, 0.0), axis=1, keepdims=True)


def attention_payload(w_query, key_matrix, value_matrix, out_turned, gain):
    rows, q_cols = w_query.shape
    kv = key_matrix.shape[1]

    def body(q, k, v, o, g, out):
        gains = column_of(g[...].astype(f32))
        low = lambda w: w[...].astype(f32) * gains
        out[...] = jnp.concatenate([low(q), low(k), o[...].astype(f32), low(v)], axis=1).astype(bf16)

    return kernel(body, [shape(rows, 2 * q_cols + 2 * kv)], w_query, key_matrix, value_matrix, out_turned, gain)[0]


def feed_forward_payload(w_gate, w_up, down_turned, gain, hs):
    rows, ff = w_gate.shape

    def body(gate, up, down, g, out):
        gains = column_of(g[...].astype(f32))
        blank = jnp.zeros((rows, LANES), bf16)
        per = hs // LANES
        for tile in range(4 * per):
            quarter, place = tile // per, tile % per
            at = tile * LANES
            gate_cols = slice(2 * place * LANES, (2 * place + 1) * LANES)
            up_cols = slice((2 * place + 1) * LANES, (2 * place + 2) * LANES)
            down_cols = slice(2 * hs + place * LANES, 2 * hs + (place + 1) * LANES)
            if at < ff:
                cols = slice(at, at + LANES)
                out[quarter, :, gate_cols] = (gate[:, cols].astype(f32) * gains).astype(bf16)
                out[quarter, :, up_cols] = (up[:, cols].astype(f32) * gains).astype(bf16)
                out[quarter, :, down_cols] = down[:, cols]
            else:
                out[quarter, :, gate_cols] = blank
                out[quarter, :, up_cols] = blank
                out[quarter, :, down_cols] = blank

    return kernel(body, [shape(4, rows, 3 * hs)], w_gate, w_up, down_turned, gain)[0]


def rotary_tables(seq_len):
    half = HEAD_SIZE // 2
    frequency = rotary_base ** (-2.0 * np.arange(half, dtype=np.float32) / HEAD_SIZE)
    angles = np.arange(seq_len, dtype=np.float32)[:, None] * frequency[None, :].astype(np.float32)
    times = 2 * LANES // HEAD_SIZE
    return np.tile(np.cos(angles), (1, times)).astype(np.float32), np.tile(np.sin(angles), (1, times)).astype(np.float32)


def turn(tile, cosine, sine):
    lane = lax.broadcasted_iota(jnp.int32, tile.shape, 1) % HEAD_SIZE
    ahead = pltpu.roll(tile, LANES - HEAD_SIZE // 2, 1)
    behind = pltpu.roll(tile, HEAD_SIZE // 2, 1)
    return tile * cosine + jnp.where(lane < HEAD_SIZE // 2, -ahead, behind) * sine


def upper_half(tile):
    lane = lax.broadcasted_iota(jnp.int32, tile.shape, 1)
    high = jnp.where(lane >= HEAD_SIZE, tile, 0.0)
    return pltpu.roll(high, HEAD_SIZE, 1).astype(bf16), high.astype(bf16)


def softmax_mask(seq_len):
    return lax.broadcasted_iota(jnp.int32, (seq_len, seq_len), 0) >= lax.broadcasted_iota(jnp.int32, (seq_len, seq_len), 1)


def place_halves(ref, core, mine, other):
    half = mine.shape[0]
    ref[pl.ds(pl.multiple_of(core * half, half), half), :] = mine[...].astype(f32)
    ref[pl.ds(pl.multiple_of((1 - core) * half, half), half), :] = other[...].astype(f32)


def attention_forward(scalars, tokens, other_tokens, chunks, order, cosine, sine, heads):
    seq_len, width = 2 * tokens.shape[0], tokens.shape[1]
    cols = chunks[0].shape[1]
    q_wide = heads * HEAD_SIZE + HEAD_SIZE
    tiles = q_wide // LANES
    n_w = len(chunks)
    scale = HEAD_SIZE ** (-0.5)

    def body(*refs):
        s, tok, tok_other, perm, cs, sn = refs[:6]
        w_in = refs[6 : 6 + n_w]
        normed_out, qk_out, v_out, att_out, lse_out, branch_top, branch_low = refs[6 + n_w : 13 + n_w]
        w, whole = refs[13 + n_w :]
        fill(w, w_in)
        place_halves(whole, s[1], tok, tok_other)
        inputs = whole[...]
        stat = lax.rsqrt(jnp.mean(inputs * inputs, axis=-1, keepdims=True) + eps)
        normed = nn((inputs * stat).astype(bf16), perm[...]).astype(bf16)
        normed_out[...] = normed
        cosines, sines = cs[...], sn[...]
        qk = nn(normed, w[:, :q_wide])
        rotated = [turn(qk[:, t * LANES : (t + 1) * LANES], cosines, sines) for t in range(tiles)]
        for t in range(tiles):
            qk_out[:, t * LANES : (t + 1) * LANES] = rotated[t].astype(bf16)
        key_low, key_high = upper_half(rotated[-1])
        value = nn(normed, w[:, cols - LANES :])
        value_low, value_high = upper_half(value)
        v_out[...] = value_high
        seen = softmax_mask(seq_len)
        for t in range(tiles):
            query = rotated[t].astype(bf16)
            total = jnp.zeros((seq_len, LANES), f32)
            for side in (0, 1):
                h = 2 * t + side
                if h >= heads:
                    continue
                scores = jnp.where(seen, nt(query, key_high if side else key_low) * scale, -1e30)
                top = jnp.max(scores, axis=-1, keepdims=True)
                grown = jnp.exp(scores - top)
                mass = jnp.sum(grown, axis=-1, keepdims=True)
                lse_out[:, h : h + 1] = top + jnp.log(mass)
                probs = (grown / mass).astype(bf16)
                total = total + nn(probs, value_high if side else value_low)
            att_out[:, t * LANES : (t + 1) * LANES] = total.astype(bf16)
        branch = nt(att_out[...], w[:, q_wide:]).astype(bf16)
        branch = nt(branch, perm[...]).astype(bf16)
        branch_top[...] = branch[: seq_len // 2]
        branch_low[...] = branch[seq_len // 2 :]

    return kernel(
        body,
        [
            shape(seq_len, width), shape(seq_len, q_wide), shape(seq_len, LANES), shape(seq_len, q_wide),
            shape(seq_len, LANES, dtype=f32), shape(seq_len // 2, width), shape(seq_len // 2, width),
        ],
        tokens, other_tokens, order, cosine, sine, *chunks,
        scalars=scalars,
        scratch=[pltpu.VMEM((width, cols), bf16), pltpu.VMEM((seq_len, width), f32)],
    )


def middle_step(scalars, tokens, other_tokens, branches, order):
    half, width = tokens.shape
    seq_len = 2 * half

    def body(s, tok, tok_other, top, low, top_other, low_other, perm, middle_out, x_out):
        active = s[0].astype(f32)
        place_halves(middle_out, s[1], tok, tok_other)
        for rows, a, b in ((slice(0, half), top, top_other), (slice(half, seq_len), low, low_other)):
            middle_out[rows, :] = middle_out[rows, :] + active * (a[...].astype(f32) + b[...].astype(f32))
        at = pl.multiple_of(s[1] * half, half)
        own = middle_out[pl.ds(at, half), :]
        stat = lax.rsqrt(jnp.mean(own * own, axis=-1, keepdims=True) + eps)
        x = nn((own * stat).astype(bf16), perm[...]).astype(bf16)
        for t in range(4):
            x_out[t, :, :] = x

    return kernel(body, [shape(seq_len, width, dtype=f32), shape(4, half, width)], tokens, other_tokens, *branches, order, scalars=scalars)


def cotangent_step(scalars, cotangent, order):
    half, width = cotangent.shape

    def body(s, cot, perm, out):
        c = nn((s[0].astype(f32) * cot[...].astype(f32)).astype(bf16), perm[...]).astype(bf16)
        for t in range(4):
            out[t, :, :] = c

    return kernel(body, [shape(4, half, width)], cotangent, order, scalars=scalars)[0]


def hidden_units(xs, gus):
    n_x, n_w = len(xs), len(gus)
    tokens = sum(x.shape[0] * x.shape[1] for x in xs)
    width = xs[0].shape[-1]
    hs = gus[0].shape[1] // 2

    def body(*refs):
        x_in, w_in = refs[:n_x], refs[n_x : n_x + n_w]
        hid, slope, x, w = refs[n_x + n_w :]
        fill(x, x_in)
        fill(w, w_in)

        def block(i, carry):
            at = pl.multiple_of(i * LANES, LANES)
            at2 = pl.multiple_of(i * 2 * LANES, 2 * LANES)
            gu = nn(x[...], w[:, pl.ds(at2, 2 * LANES)])
            gate, up = gu[:, :LANES], gu[:, LANES:]
            sig = 1.0 / (1.0 + jnp.exp(-gate))
            act = gate * sig
            hid[:, pl.ds(at, LANES)] = (act * up).astype(bf16)
            slope[:, pl.ds(at2, LANES)] = (up * sig * (1.0 + gate * (1.0 - sig))).astype(bf16)
            slope[:, pl.ds(pl.multiple_of(at2 + LANES, LANES), LANES)] = act.astype(bf16)
            return carry

        lax.fori_loop(0, hs // LANES, block, 0)

    return kernel(
        body,
        [shape(tokens, hs), shape(tokens, 2 * hs)],
        *xs, *gus,
        scratch=[pltpu.VMEM((tokens, width), bf16), pltpu.VMEM((width, 2 * hs), bf16)],
    )


def hidden_back(cs, slope, gus, downs):
    n_x, n_w = len(cs), len(gus)
    tokens = slope.shape[0]
    half = tokens // 2
    width = cs[0].shape[-1]
    hs = downs[0].shape[1]

    def body(*refs):
        c_in, slope_r = refs[:n_x], refs[n_x]
        g_in, d_in = refs[n_x + 1 : n_x + 1 + n_w], refs[n_x + 1 + n_w : n_x + 1 + 2 * n_w]
        e_mine, e_away, dgu, c, wg, wd = refs[n_x + 1 + 2 * n_w :]
        fill(c, c_in)
        fill(wd, d_in)
        fill(wg, g_in)

        def block(i, carry):
            at = pl.multiple_of(i * LANES, LANES)
            at2 = pl.multiple_of(i * 2 * LANES, 2 * LANES)
            at3 = pl.multiple_of(at2 + LANES, LANES)
            dh = nn(c[...], wd[:, pl.ds(at, LANES)])
            dgu[:, pl.ds(at2, LANES)] = (dh * slope_r[:, pl.ds(at2, LANES)].astype(f32)).astype(bf16)
            dgu[:, pl.ds(at3, LANES)] = (dh * slope_r[:, pl.ds(at3, LANES)].astype(f32)).astype(bf16)
            return carry

        lax.fori_loop(0, hs // LANES, block, 0)

        def rows_of(out, base):
            for q in range(half // 256):
                piece = nt(dgu[base + q * 256 : base + (q + 1) * 256, :], wg[...]).astype(bf16)
                out[2 * q, :, :] = piece[:128]
                out[2 * q + 1, :, :] = piece[128:]

        rows_of(e_away, half)
        rows_of(e_mine, 0)

    quads = shape(4, half // 4, width)
    return kernel(
        body,
        [quads, quads, shape(tokens, 2 * hs)],
        *cs, slope, *gus, *downs,
        scratch=[pltpu.VMEM((tokens, width), bf16), pltpu.VMEM((width, 2 * hs), bf16), pltpu.VMEM((width, hs), bf16)],
    )


def weight_grads(lefts, right, parts):
    n_x = len(lefts)
    tokens, cols = right.shape
    width = lefts[0].shape[-1]
    h = width // 2
    each = cols // parts

    def body(*refs):
        right_r, outs, x = refs[n_x], refs[n_x + 1 : n_x + 1 + 2 * parts], refs[n_x + 1 + 2 * parts]
        fill(x, refs[:n_x])

        def step(i, carry):
            at = pl.multiple_of(i * LANES, LANES)
            for p in range(parts):
                whole = tn(x[...], right_r[:, pl.ds(pl.multiple_of((i * parts + p) * LANES, LANES), LANES)]).astype(bf16)
                outs[2 * p][:, pl.ds(at, LANES)] = whole[:h]
                outs[2 * p + 1][:, pl.ds(at, LANES)] = whole[h:]
            return carry

        lax.fori_loop(0, each // LANES, step, 0)

    return kernel(body, [shape(h, each)] * (2 * parts), *lefts, right, scratch=[pltpu.VMEM((tokens, width), bf16)])


def ff_output(hid, downs):
    tokens, hs = hid.shape
    n_w = len(downs)
    width = sum(d.shape[0] for d in downs)
    half = tokens // 2

    def body(*refs):
        hid_r, d_in = refs[0], refs[1 : 1 + n_w]
        mine, away, wd = refs[1 + n_w :]
        fill(wd, d_in)
        for out, base in ((away, half), (mine, 0)):
            for q in range(half // 256):
                piece = nt(hid_r[base + q * 256 : base + (q + 1) * 256, :], wd[...]).astype(bf16)
                out[2 * q, :, :] = piece[:128]
                out[2 * q + 1, :, :] = piece[128:]

    quads = shape(4, half // 4, width)
    return kernel(body, [quads, quads], hid, *downs, scratch=[pltpu.VMEM((width, hs), bf16)])


def add_pair(mine, other):
    return (mine.astype(f32) + other.astype(f32)).astype(bf16)


def sum_natural(parts, order):
    _, rows, width = parts.shape

    def body(p, perm, out):
        total = p[0].astype(f32) + p[1].astype(f32) + p[2].astype(f32) + p[3].astype(f32)
        out[...] = nt(total.astype(bf16), perm[...]).astype(bf16)

    return kernel(body, [shape(rows, width)], parts, order)[0]


def output_step(scalars, parts, order, middle):
    _, rows, width = parts.shape

    def body(s, p, perm, mid, out):
        total = p[0].astype(f32) + p[1].astype(f32) + p[2].astype(f32) + p[3].astype(f32)
        own = mid[pl.ds(pl.multiple_of(s[1] * rows, rows), rows), :]
        out[...] = (own + s[0].astype(f32) * nt(total.astype(bf16), perm[...])).astype(bf16)

    return kernel(body, [shape(rows, width)], parts, order, middle, scalars=scalars)[0]


def attention_backward(scalars, e_mine, e_other, cot, other_cot, middle, order, cosine, sine, normed, qk, value, attended, lse, chunks, heads):
    seq_len, width = middle.shape
    half = seq_len // 2
    cols = chunks[0].shape[1]
    q_wide = heads * HEAD_SIZE + HEAD_SIZE
    tiles = q_wide // LANES
    n_w = len(chunks)
    scale = HEAD_SIZE ** (-0.5)

    def body(*refs):
        s, em, eo, co, co_other, mid, perm, cs, sn, nrm, qk_r, v_r, att, lse_r = refs[:14]
        w_in = refs[14 : 14 + n_w]
        dw_outs = refs[14 + n_w : 18 + n_w]
        e_keep, e_away, dmid_out = refs[18 + n_w : 21 + n_w]
        w, e_all, dqk, whole_e = refs[21 + n_w :]
        fill(w, w_in)
        core = s[1]
        active = s[0].astype(f32)
        mine_at = pl.multiple_of(core * half, half)
        other_at = pl.multiple_of((1 - core) * half, half)
        place_halves(e_all, core, em, eo)
        place_halves(whole_e, core, co, co_other)
        middles = mid[...]
        stat = lax.rsqrt(jnp.mean(middles * middles, axis=-1, keepdims=True) + eps)
        scaled = middles * stat
        e = e_all[...]
        d_middle = whole_e[...] + stat * (e - scaled * jnp.mean(e * scaled, axis=-1, keepdims=True))
        e_all[...] = d_middle
        dmid_out[...] = e_all[pl.ds(mine_at, half), :]
        d_branch = nn((active * d_middle).astype(bf16), perm[...]).astype(bf16)
        d_att = nn(d_branch, w[:, q_wide:]).astype(bf16)
        key_low, key_high = upper_half(qk_r[:, q_wide - LANES :].astype(f32))
        value_low, value_high = upper_half(v_r[...].astype(f32))
        seen = softmax_mask(seq_len)
        d_key = [jnp.zeros((seq_len, LANES), f32), jnp.zeros((seq_len, LANES), f32)]
        d_value = [jnp.zeros((seq_len, LANES), f32), jnp.zeros((seq_len, LANES), f32)]
        cosines, sines = cs[...], -sn[...]
        last = None
        for t in range(tiles):
            query = qk_r[:, t * LANES : (t + 1) * LANES]
            da = d_att[:, t * LANES : (t + 1) * LANES]
            total = jnp.zeros((seq_len, LANES), f32)
            for side in (0, 1):
                h = 2 * t + side
                if h >= heads:
                    continue
                key = key_high if side else key_low
                scores = jnp.where(seen, nt(query, key) * scale, -1e30)
                probs = jnp.exp(scores - lse_r[:, h : h + 1])
                d_probs = nt(da, value_high if side else value_low)
                d_value[side] = d_value[side] + tn(probs.astype(bf16), da)
                d_scores = (probs * (d_probs - jnp.sum(probs * d_probs, axis=-1, keepdims=True))).astype(bf16)
                total = total + nn(d_scores, key)
                d_key[side] = d_key[side] + tn(d_scores, query)
            if t < tiles - 1:
                dqk[:, t * LANES : (t + 1) * LANES] = turn(total * scale, cosines, sines).astype(bf16)
            else:
                last = total
        lane = lax.broadcasted_iota(jnp.int32, (seq_len, LANES), 1)
        low_lane = lane < HEAD_SIZE
        key_total = jnp.where(low_lane, last, d_key[1] + pltpu.roll(d_key[0], HEAD_SIZE, 1))
        dqk[:, q_wide - LANES :] = turn(key_total * scale, cosines, sines).astype(bf16)
        dv = jnp.where(low_lane, 0.0, d_value[1] + pltpu.roll(d_value[0], HEAD_SIZE, 1)).astype(bf16)
        normed_t = nrm[...]
        d_all = dqk[...]
        first = tn(normed_t, d_all)
        second = tn(d_branch, att[...])
        third = tn(normed_t, dv)
        quarter = width // 4
        for q in range(4):
            rows = slice(q * quarter, (q + 1) * quarter)
            dw_outs[q][:, :q_wide] = first[rows].astype(bf16)
            dw_outs[q][:, q_wide : cols - LANES] = second[rows, : q_wide - LANES].astype(bf16)
            dw_outs[q][:, cols - LANES :] = (second[rows, q_wide - LANES :] + third[rows]).astype(bf16)
        e_one = (nt(d_all, w[:, :q_wide]) + nt(dv, w[:, cols - LANES :])).astype(bf16)
        whole_e[...] = nt(e_one, perm[...])
        e_keep[...] = whole_e[pl.ds(mine_at, half), :]
        e_away[...] = whole_e[pl.ds(other_at, half), :].astype(bf16)

    return kernel(
        body,
        [shape(width // 4, cols)] * 4 + [shape(half, width, dtype=f32), shape(half, width), shape(half, width, dtype=f32)],
        e_mine, e_other, cot, other_cot, middle, order, cosine, sine, normed, qk, value, attended, lse, *chunks,
        scalars=scalars,
        scratch=[
            pltpu.VMEM((width, cols), bf16), pltpu.VMEM((seq_len, width), f32),
            pltpu.VMEM((seq_len, q_wide), bf16), pltpu.VMEM((seq_len, width), f32),
        ],
    )


def tokens_step(tokens, e_keep, e_other, d_middle):
    def body(tok, keep, other, dm, out):
        inputs = tok[...].astype(f32)
        stat = lax.rsqrt(jnp.mean(inputs * inputs, axis=-1, keepdims=True) + eps)
        scaled = inputs * stat
        e = keep[...] + other[...].astype(f32)
        out[...] = (dm[...] + stat * (e - scaled * jnp.mean(e * scaled, axis=-1, keepdims=True))).astype(bf16)

    return kernel(body, [shape(*tokens.shape)], tokens, e_keep, e_other, d_middle)[0]


def on_device(
    tokens, cotangent, parents, skip, w_query, key_matrix, value_matrix, w_out, w_gate, w_up, w_down, gain_attn, gain_mlp
):
    half_rows, width = tokens.shape
    seq_len = 2 * half_rows
    rows = w_query.shape[0]
    n1 = lax.axis_size("z1")
    q_cols = w_query.shape[1]
    kv_cols = key_matrix.shape[1]
    heads = q_cols // HEAD_SIZE
    ff = w_gate.shape[1]
    hs = -(-ff // (4 * LANES)) * LANES
    core = lax.axis_index("tp")
    scalars = jnp.stack([1 - skip[0], core.astype(jnp.int32)])
    cos_np, sin_np = rotary_tables(seq_len)
    cosine, sine = jnp.asarray(cos_np), jnp.asarray(sin_np)
    gain_one = gain_attn.astype(f32)[:, None]
    gain_two = gain_mlp.astype(f32)[:, None]

    attn_own = attention_payload(w_query, key_matrix, value_matrix, w_out.T, gain_attn[None, :])
    ff_in = after((w_gate, w_up, w_down.T), attn_own)
    ff_blocks = feed_forward_payload(*ff_in, gain_mlp[None, :], hs)
    other_tokens = swap(tokens, "tp")
    other_cot = swap(cotangent, "tp")
    natural = lax.broadcasted_iota(jnp.int32, (width, 1), 0)
    to_hidden = (natural == natural_of(n1, rows, ("y", "z1", "z0", "x"), ("y", "z1"))).astype(bf16)
    to_attn = (natural == natural_of(n1, rows, ("y", "x", "z1", "z0"), ("y", "x", "z1", "z0"))).astype(bf16)
    c_wide = cotangent_step(scalars, cotangent, to_hidden)
    attn_line = after(gather_line(attn_own), to_hidden, to_attn, c_wide, other_tokens, other_cot)
    ff_t = exchange(ff_blocks, T_AXES).reshape(4 * rows, 3 * hs)
    gu_t, down_t = ff_t[:, : 2 * hs], ff_t[:, 2 * hs :]

    line_y = swap(attn_line, "y")
    attn_w = [attn_line, swap(attn_line, "x"), line_y, swap(line_y, "x")]
    two = n1 == 2
    if two:
        gu_z, gu_y = swap(gu_t, "z1"), swap(gu_t, "y")
        other_tokens, c_wide = after((other_tokens, c_wide), attn_w, gu_z, gu_y)

    own_c = exchange(c_wide, T_AXES)
    normed, qk, value, attended, lse, *branch = attention_forward(scalars, tokens, other_tokens, attn_w, to_attn, cosine, sine, heads)
    branch = branch + [swap(b, "tp") for b in branch]
    if two:
        gu_zy, down_z = swap(gu_z, "y"), swap(down_t, "z1")
        branch = after(branch, gu_zy, down_z, own_c)
    middle, x_wide = middle_step(scalars, tokens, other_tokens, branch, to_hidden)
    own_x = exchange(x_wide, T_AXES)
    if two:
        down_y, down_zy = swap(after(down_t, x_wide), "y"), swap(after(down_z, x_wide), "y")
        own_x = after(own_x, down_y, down_zy)
        gus = [gu_t, gu_z, gu_y, gu_zy]
        downs = [down_t, down_z, down_y, down_zy]
    else:
        gu_all, down_all = (lax.all_gather(v, "z1", axis=0, tiled=True) for v in (gu_t, down_t))
        gus, downs = [gu_all, swap(gu_all, "y")], [down_all, swap(down_all, "y")]
    xs = [own_x, swap(own_x, "tp")]
    cs = [own_c, swap(after(own_c, x_wide), "tp")]

    hidden, slope = hidden_units(xs, gus)
    d_own, d_other = weight_grads(cs, hidden, 1)
    e_keep, e_away, d_gu = hidden_back(cs, after(slope, d_other), gus, downs)
    e_sum = add_pair(e_keep, swap(e_away, "tp"))
    e_parts = exchange(e_sum, T_AXES)
    gate_own, gate_other, up_own, up_other = weight_grads(xs, after(d_gu, e_sum), 2)
    m_keep, m_away = ff_output(after(hidden, up_other), downs)
    e_mine = sum_natural(after(e_parts, m_keep), to_hidden)
    m_sum = add_pair(m_keep, swap(m_away, "tp"))
    m_parts = exchange(after(m_sum, e_mine), T_AXES)
    half_down = reduce_y(d_own, d_other)
    e_mine = after(e_mine, half_down)

    dw_parts = attention_backward(
        scalars, e_mine, swap(e_mine, "tp"), cotangent, other_cot, middle, to_attn, cosine, sine, normed, qk, value, attended, lse, attn_w, heads
    )
    e1_keep, e1_away, d_middle = dw_parts[4:]
    far = (dw_parts[2].astype(f32) + swap(dw_parts[3], "x").astype(f32)).astype(bf16)
    line_sum = dw_parts[0].astype(f32) + swap(dw_parts[1], "x").astype(f32) + swap(far, "y").astype(f32)
    line_sum = line_sum.astype(bf16)
    output = output_step(scalars, after(m_parts, line_sum), to_hidden, middle)

    halves = [half_down, reduce_y(after(gate_own, dw_parts), gate_other), reduce_y(after(up_own, dw_parts), up_other)]
    if two:
        mine = [h[: 4 * rows] for h in halves]
        from_z = after([swap(h[4 * rows :], "z1") for h in halves], line_sum)
        summed = [(a.astype(f32) + b.astype(f32)).astype(bf16) for a, b in zip(mine, from_z)]
    else:
        summed = [
            jnp.sum(exchange(h.reshape(n1, 4 * rows, hs), "z1").astype(f32), axis=0).astype(bf16) for h in halves
        ]
    got_ff = exchange(after(jnp.concatenate(summed, axis=1).reshape(4, rows, 3 * hs), m_parts), T_AXES)
    if two:
        parts = line_sum.reshape(4, rows, -1)
        owned = parts[0].astype(f32)
        for k in (1, 2, 3):
            owned = owned + lax.ppermute(parts[k], ("z1", "z0"), [(i, i ^ k) for i in range(4)]).astype(f32)
    else:
        got = jnp.sum(exchange(line_sum.reshape(n1, 2, rows, -1), "z1").astype(f32), axis=0)
        owned = got[0] + swap(got[1].astype(bf16), "z0").astype(f32)
    grad_tokens = tokens_step(tokens, e1_keep, swap(e1_away, "tp"), d_middle)

    whole = lambda got: got.astype(f32).transpose(1, 0, 2).reshape(rows, 4 * hs)[:, :ff]
    down_s, dg_scaled, du_scaled = (whole(got_ff[:, :, k * hs : (k + 1) * hs]) for k in range(3))
    grad_w_down = down_s.T

    dq_s = owned[:, :q_cols]
    dk_s = owned[:, q_cols : q_cols + kv_cols]
    d_out = owned[:, q_cols + kv_cols : 2 * q_cols + kv_cols]
    dv_s = owned[:, 2 * q_cols + kv_cols :]
    row_sum = lambda w, d: jnp.sum(w.astype(f32) * d, axis=1)
    gain_parts = jnp.stack(
        [
            row_sum(w_query, dq_s) + row_sum(key_matrix, dk_s) + row_sum(value_matrix, dv_s),
            row_sum(w_gate, dg_scaled) + row_sum(w_up, du_scaled),
        ]
    )
    gains = gain_parts + swap(gain_parts, "tp")
    return (
        output,
        grad_tokens,
        dq_s * gain_one,
        dk_s * gain_one,
        dv_s * gain_one,
        d_out.T,
        dg_scaled * gain_two,
        du_scaled * gain_two,
        grad_w_down,
        gains[0],
        gains[1],
    )


def solution(mesh):
    n1 = mesh.shape["fsdp"] // 8
    fine = Mesh(mesh.devices.reshape(n1, 2, 2, 2, mesh.shape["tp"]), ("z1", "z0", "y", "x", "tp"))
    fs = ("z1", "z0", "y", "x")
    both = fs + ("tp",)
    in_specs = (
        P(both, None), P(both, None), P(fs, None), P(fs),
        P(fs, "tp"), P(fs, "tp"), P(fs, "tp"), P("tp", fs),
        P(fs, "tp"), P(fs, "tp"), P("tp", fs), P(fs), P(fs),
    )
    out_specs = (
        P(both, None), P(both, None), P(fs, "tp"), P(fs, "tp"), P(fs, "tp"), P("tp", fs),
        P(fs, "tp"), P(fs, "tp"), P("tp", fs), P(fs), P(fs),
    )
    return jax.shard_map(on_device, mesh=fine, in_specs=in_specs, out_specs=out_specs, check_vma=False)
```

time: 288 us -> 257 us (0.89)
  Pallas kernels: 0 us -> 77.9 us
  matrix products: 32.9 us -> 0 us
  other arithmetic: 48.4 us -> 16.6 us
  local copies, waits for them, and re-layouts: 34.7 us -> 7.08 us
  blocking collectives: 11.1 us -> 0 us
  waiting for transfers between devices: 96.4 us -> 90 us
    pallas_call x0 -> x15, Pallas kernels: none -> 77.9 us  [kernel(): pl.pallas_call(body, out_shape=list(outs), in_specs=specs, out_specs=[who...]
    all_to_all x7 -> x6, waiting for transfers between devices: 44.2 us -> 2.16 us  [exchange(): return lax.all_to_all(blocks, axes, 0, 0, tiled=True)]
    dot_general x22 -> x0, matrix products: 32.9 us -> none  [the longest x6 10.6 us: nt(): lax.dot_general(a, b, (((1,), (1,)), ((), ())), preferred_element_type=f32)]
    ppermute x18 -> x29, waiting for transfers between devices: 42 us -> 68 us  [swap(): return lax.ppermute(value, axis, SWAP)]
    ppermute x18 -> x29, starting transfers between devices: 13 us -> 29.5 us  [swap(): return lax.ppermute(value, axis, SWAP)]
    another operation x12 -> x1, other arithmetic: 15.1 us -> 0.59 us  [on_device(): scalars = jnp.stack([1 - skip[0], core.astype(jnp.int32)])]
    all_to_all x1 -> x0, blocking collectives: 11.1 us -> none  [on_device(): lax.all_to_all(gate_up, T_AXES, 0, 0, tiled=True).reshape(4 * rows, 2 * hs)]
    dot_general x4 -> x0, local copies, waits for them, and re-layouts: 10.5 us -> none  [tn(): lax.dot_general(a, b, (((0,), (0,)), ((), ())), preferred_element_type=f32)]
  transfers between devices with their start and end apart: 37 -> 41, of which waited for: 12 -> 22; matrix products, arithmetic and copies ran while one was open for 31% -> 5% of each run, Pallas kernels for 0% -> 21%
where the time goes in v2:
time: 257 us; the launch traced here: 256 us
  waiting for transfers between devices  90 us (35%)
  Pallas kernels  77.9 us (30%)
  starting transfers between devices  62.3 us (24%)
  other arithmetic  16.6 us (6%)
  local copies, waits for them, and re-layouts  7.08 us (3%)
    pallas_call x15, Pallas kernels, kernel(): pl.pallas_call(body, out_shape=list(outs), in_specs=specs, out_specs=[who...  77.9 us
    ppermute x29, waiting for transfers between devices, swap(): return lax.ppermute(value, axis, SWAP)  68 us
    ppermute x29, starting transfers between devices, swap(): return lax.ppermute(value, axis, SWAP)  29.5 us
    all_to_all x6, starting transfers between devices, exchange(): return lax.all_to_all(blocks, axes, 0, 0, tiled=True)  23.7 us
    ppermute x3, waiting for transfers between devices, on_device(): lax.ppermute(parts[k], ('z1', 'z0'), [(i, i ^ k) for i in range(4)])  11.9 us
    ppermute x3, waiting for transfers between devices, others(): lax.ppermute(value, axes, [(i, i ^ k) for i in range(4)])  7.98 us
    unnamed x83, local copies, waits for them, and re-layouts  5.61 us
  transfers between devices with their start and end apart: 41, of which 22 were waited for; matrix products, arithmetic and copies ran while one was open for 5% of the time, Pallas kernels for 21%

profile of v2, /device:TPU:0, one launch (start us, length us, event | category | flops | bytes accessed | tf_op | source)
XLA Modules:
  0.0 255.8 jit_solution(6142202651253308085)
XLA Ops:
  2.3 2.3 shard_map.224
  4.6 5.2 %all-to-all-start = ((bf16[4,56,1920]{2,1,0:T(8,128)(2,1)}), bf16[4,56,1920]{2,1,0:T(8,128)(2,1)S(1)}, u32[]{:S(2)}, u32[]{:S(2)}) async-start(bf16[4,56,1920]{2,1,0:T(8,128)(2,1)} %shard_map.224), calls=%async_computation | async-start | bytes 1720320 | tf_op jit(solution)/shard_map/all_to_all | solution.py:41
  9.8 2.0 collective-permute-start.1
  11.9 2.6 %collective-permute-start.2 = (bf16[56,1024]{1,0:T(8,128)(2,1)S(1)}, bf16[56,1024]{1,0:T(8,128)(2,1)S(1)}, u32[]{:S(2)}, u32[]{:S(2)}) collective-permute-start(bf16[56,1024]{1,0:T(8,128)(2,1)S(1)} %copy-done.25), channel_id=1, source_target_pairs={{0,16},{8,24},{16,0},{24,8},{1,17},{9,25},{17,1},{25,9},{2,18},{10... | collective-permute-start | bytes 344072 | tf_op jit(solution)/shard_map/ppermute | solution.py:45
  16.3 1.7 fusion.perm
  18.1 1.8 fusion.1.refs_3_.refs_6_
  19.9 3.0 %shard_map.221 = bf16[4,128,896]{2,1,0:T(8,128)(2,1)} custom-call(s32[2]{0:T(128)} %pad_add_fusion.s.refs_0_, bf16[128,896]{1,0:T(8,128)(2,1)} %refs_3_.1, bf16[896,896]{1,0:T(8,128)(2,1)} %fusion.perm), custom_call_target="tpu_custom_call" | custom-call | flops 1000 | bytes 1000 | tf_op jit(solution)/shard_map/pallas_call | solution.py:58
  22.9 3.5 %collective-permute-done.1.refs_1_ = bf16[56,1024]{1,0:T(8,128)(2,1)S(1)} collective-permute-done((bf16[56,1024]{1,0:T(8,128)(2,1)S(1)}, bf16[56,1024]{1,0:T(8,128)(2,1)S(1)}, u32[]{:S(2)}, u32[]{:S(2)}) %collective-permute-start.1) | collective-permute-done | bytes 114720 | tf_op jit(solution)/shard_map/ppermute | solution.py:45
  26.4 4.5 %collective-permute-done.3.refs_3_ = bf16[56,1024]{1,0:T(8,128)(2,1)S(1)} collective-permute-done((bf16[56,1024]{1,0:T(8,128)(2,1)S(1)}, bf16[56,1024]{1,0:T(8,128)(2,1)S(1)}, u32[]{:S(2)}, u32[]{:S(2)}) %collective-permute-start.3) | collective-permute-done | bytes 114720 | tf_op jit(solution)/shard_map/ppermute | solution.py:45
  31.5 1.9 shard_map.223.refs_6_.refs_14_
  37.9 9.8 %collective-permute-done.6.refs_8_.refs_16_ = bf16[224,1024]{1,0:T(8,128)(2,1)S(1)} collective-permute-done((bf16[224,1024]{1,0:T(8,128)(2,1)}, bf16[224,1024]{1,0:T(8,128)(2,1)S(1)}, u32[]{:S(2)}, u32[]{:S(2)}) %collective-permute-start.6) | collective-permute-done | bytes 458784 | tf_op jit(solution)/shard_map/ppermute | solution.py:32
  49.2 7.8 %collective-permute-done.7.refs_9_.refs_17_ = bf16[224,1024]{1,0:T(8,128)(2,1)S(1)} collective-permute-done((bf16[224,1024]{1,0:T(8,128)(2,1)S(1)}, bf16[224,1024]{1,0:T(8,128)(2,1)S(1)}, u32[]{:S(2)}, u32[]{:S(2)}) %collective-permute-start.7) | collective-permute-done | bytes 458784 | tf_op jit(solution)/shard_map/ppermute | solution.py:32
  57.0 3.0 %collective-permute-done.8.refs_3_.refs_4_ = bf16[224,1280]{1,0:T(8,128)(2,1)S(1)} collective-permute-done((bf16[224,1280]{1,0:T(8,128)(2,1)S(1)}, bf16[224,1280]{1,0:T(8,128)(2,1)S(1)}, u32[]{:S(2)}, u32[]{:S(2)}) %collective-permute-start.8) | collective-permute-done | bytes 573472 | tf_op jit(solution)/shard_map/ppermute | solution.py:32
  60.1 3.5 %all-to-all-start.1 = ((bf16[4,128,896]{2,1,0:T(8,128)(2,1)}), bf16[4,128,896]{2,1,0:T(8,128)(2,1)S(1)}, u32[]{:S(2)}, u32[]{:S(2)}) async-start(bf16[4,128,896]{2,1,0:T(8,128)(2,1)} %shard_map.221), calls=%async_computation.1 | async-start | bytes 1835008 | tf_op jit(solution)/shard_map/all_to_all | solution.py:41
  66.0 6.8 %shard_map.225 = (bf16[256,896]{1,0:T(8,128)(2,1)}, bf16[256,512]{1,0:T(8,128)(2,1)}, bf16[256,128]{1,0:T(8,128)(2,1)}, bf16[256,512]{1,0:T(8,128)(2,1)}, f32[25...) custom-call(s32[2]{0:T(128)} %pad_add_fusion.s.refs_0_, bf16[128,896]{1,0:T(8,128)(2,1)} %tok.3, ...), custom_call_target="tpu_custom_call" | custom-call | flops 1000 | bytes 1000 | tf_op jit(solution)/shard_map/pallas_call | solution.py:58
  73.5 6.8 %collective-permute-done.13.refs_8_.refs_2_ = bf16[224,640]{1,0:T(8,128)(2,1)S(1)} collective-permute-done((bf16[224,640]{1,0:T(8,128)(2,1)S(1)}, bf16[224,640]{1,0:T(8,128)(2,1)S(1)}, u32[]{:S(2)}, u32[]{:S(2)}) %collective-permute-start.13) | collective-permute-done | bytes 286752 | tf_op jit(solution)/shard_map/ppermute | solution.py:32
  80.3 2.1 all-to-all-done.1.refs_0_
  82.4 4.1 %shard_map.226 = (f32[256,896]{1,0:T(8,128)}, bf16[4,128,896]{2,1,0:T(8,128)(2,1)}) custom-call(s32[2]{0:T(128)} %pad_add_fusion.s.refs_0_, bf16[128,896]{1,0:T(8,128)(2,1)} %tok.3, bf16[128,896]{1,0:T(8,128)(2,1)} %copy-done.18, bf16[128,896]{1,0:T(8,128)(2,1)} %get-tuple-element.75.top, bf16[128,896]{1,0:T(8,128)(2,1)} %get-tuple-element.76.low, ...), custom_call_target="tpu_custom_call" | custom-call | flops 1000 | bytes 1000 | tf_op jit(solution)/shard_map/pallas_call | solution.py:58
  86.5 3.7 %all-to-all-start.2 = ((bf16[4,128,896]{2,1,0:T(8,128)(2,1)}), bf16[4,128,896]{2,1,0:T(8,128)(2,1)S(1)}, u32[]{:S(2)}, u32[]{:S(2)}) async-start(bf16[4,128,896]{2,1,0:T(8,128)(2,1)} %get-tuple-element.79), calls=%async_computation.2 | async-start | bytes 1835008 | tf_op jit(solution)/shard_map/all_to_all | solution.py:41
  92.3 7.7 %collective-permute-done.15.refs_10_.refs_4_ = bf16[224,640]{1,0:T(8,128)(2,1)S(1)} collective-permute-done((bf16[224,640]{1,0:T(8,128)(2,1)S(1)}, bf16[224,640]{1,0:T(8,128)(2,1)S(1)}, u32[]{:S(2)}, u32[]{:S(2)}) %collective-permute-start.15) | collective-permute-done | bytes 286752 | tf_op jit(solution)/shard_map/ppermute | solution.py:32
  100.1 4.3 %collective-permute-done.14.refs_9_.refs_3_ = bf16[224,640]{1,0:T(8,128)(2,1)S(1)} collective-permute-done((bf16[224,640]{1,0:T(8,128)(2,1)S(1)}, bf16[224,640]{1,0:T(8,128)(2,1)S(1)}, u32[]{:S(2)}, u32[]{:S(2)}) %collective-permute-start.14) | collective-permute-done | bytes 286752 | tf_op jit(solution)/shard_map/ppermute | solution.py:32
  104.9 2.5 collective-permute-done.16.refs_1_
  107.4 8.2 %shard_map.227 = (bf16[1024,640]{1,0:T(8,128)(2,1)}, bf16[1024,1280]{1,0:T(8,128)(2,1)}) custom-call(bf16[4,128,896]{2,1,0:T(8,128)(2,1)} %copy-done.1, bf16[4,128,896]{2,1,0:T(8,128)(2,1)} %collective-permute-done.16.refs_1_, bf16[224,1280]{1,0:T(8,128)(2,1)} %copy-done.2, bf16[224,1280]{1,0:T(8,128)(2,1)} %copy-done.7, bf16[224,1280]{1,0:T(8,128)(2,1)} %copy-done.8, ...), custom_call_target="tpu_custom_call" | custom-call | flops 1000 | bytes 1000 | tf_op jit(solution)/shard_map/pallas_call | solution.py:58
  116.6 6.4 %shard_map.228 = (bf16[448,640]{1,0:T(8,128)(2,1)}, bf16[448,640]{1,0:T(8,128)(2,1)}) custom-call(bf16[4,128,896]{2,1,0:T(8,128)(2,1)} %copy-done, bf16[4,128,896]{2,1,0:T(8,128)(2,1)} %copy-done.5, bf16[1024,640]{1,0:T(8,128)(2,1)} %get-tuple-element.93.refs_2_.refs_0_), custom_call_target="tpu_custom_call" | custom-call | flops 1000 | bytes 1000 | tf_op jit(solution)/shard_map/pallas_call | solution.py:58
  123.0 10.9 %shard_map.229 = (bf16[4,128,896]{2,1,0:T(8,128)(2,1)}, bf16[4,128,896]{2,1,0:T(8,128)(2,1)}, bf16[1024,1280]{1,0:T(8,128)(2,1)}) custom-call(bf16[4,128,896]{2,1,0:T(8,128)(2,1)} %copy-done, bf16[4,128,896]{2,1,0:T(8,128)(2,1)} %copy-done.5, bf16[1024,1280]{1,0:T(8,128)(2,1)} %get-tuple-element.87.refs_2_, bf16[224,1280]{1,0:T(8,128)(2,1)} %copy-done.2, ...), custom_call_target="tpu_custom_call" | custom-call | flops 1000 | bytes 1000 | tf_op jit(solution)/shard_map/pallas_call | solution.py:58
  134.0 2.5 collective-permute-done.18
  136.6 2.4 add_convert_fusion.1
  139.0 3.7 %all-to-all-start.3 = ((bf16[4,128,896]{2,1,0:T(8,128)(2,1)}), bf16[4,128,896]{2,1,0:T(8,128)(2,1)S(1)}, u32[]{:S(2)}, u32[]{:S(2)}) async-start(bf16[4,128,896]{2,1,0:T(8,128)(2,1)} %add_convert_fusion.1), calls=%async_computation.3 | async-start | bytes 1835008 | tf_op jit(solution)/shard_map/all_to_all | solution.py:41
  143.7 9.5 %shard_map.230 = (bf16[448,640]{1,0:T(8,128)(2,1)}, bf16[448,640]{1,0:T(8,128)(2,1)}, bf16[448,640]{1,0:T(8,128)(2,1)}, bf16[448,640]{1,0:T(8,128)(2,1)}) custom-call(bf16[4,128,896]{2,1,0:T(8,128)(2,1)} %copy-done.1, bf16[4,128,896]{2,1,0:T(8,128)(2,1)} %collective-permute-done.16.refs_1_, bf16[1024,1280]{1,0:T(8,128)(2,1)} %get-tuple-element.91.refs_2_), custom_call_target="tpu_custom_call" | custom-call | flops 1000 | bytes 1000 | tf_op jit(solution)/shard_map/pallas_call | solution.py:58
  153.3 4.5 %shard_map.231 = (bf16[4,128,896]{2,1,0:T(8,128)(2,1)}, bf16[4,128,896]{2,1,0:T(8,128)(2,1)}) custom-call(bf16[1024,640]{1,0:T(8,128)(2,1)} %get-tuple-element.93.refs_2_.refs_0_, bf16[224,640]{1,0:T(8,128)(2,1)} %copy-done.6, bf16[224,640]{1,0:T(8,128)(2,1)} %copy-done.13, bf16[224,640]{1,0:T(8,128)(2,1)} %copy-done.15, bf16[224,640]{1,0:T(8,128)(2,1)} %copy-done.14), custom_call_target="tpu_custom_call" | custom-call | flops 1000 | bytes 1000 | tf_op jit(solution)/shard_map/pallas_call | solution.py:58
  158.9 3.0 %shard_map.232.refs_1_ = bf16[128,896]{1,0:T(8,128)(2,1)} custom-call(bf16[4,128,896]{2,1,0:T(8,128)(2,1)} %copy-done.4, bf16[896,896]{1,0:T(8,128)(2,1)} %fusion.perm), custom_call_target="tpu_custom_call" | custom-call | flops 1000 | bytes 1000 | tf_op jit(solution)/shard_map/pallas_call | solution.py:58
  164.4 10.2 %shard_map.233 = (bf16[224,1024]{1,0:T(8,128)(2,1)}, bf16[224,1024]{1,0:T(8,128)(2,1)}, bf16[224,1024]{1,0:T(8,128)(2,1)}, bf16[224,1024]{1,0:T(8,128)(2,1)}, f3...) custom-call(s32[2]{0:T(128)} %pad_add_fusion.s.refs_0_, bf16[128,896]{1,0:T(8,128)(2,1)} %shard_map.232.refs_1_, ...), custom_call_target="tpu_custom_call" | custom-call | flops 1000 | bytes 1000 | tf_op jit(solution)/shard_map/pallas_call | solution.py:58
  174.6 1.9 collective-permute-start.23
  178.3 2.4 collective-permute-start.29
  182.8 3.6 %all-to-all-start.4 = ((bf16[4,128,896]{2,1,0:T(8,128)(2,1)}), bf16[4,128,896]{2,1,0:T(8,128)(2,1)S(1)}, u32[]{:S(2)}, u32[]{:S(2)}) async-start(bf16[4,128,896]{2,1,0:T(8,128)(2,1)} %add_convert_fusion), calls=%async_computation.4 | async-start | bytes 1835008 | tf_op jit(solution)/shard_map/all_to_all | solution.py:41
  186.5 2.0 collective-permute-start.22
  192.7 4.6 %collective-permute-start.33 = (bf16[224,640]{1,0:T(8,128)(2,1)S(1)}, bf16[224,640]{1,0:T(8,128)(2,1)S(1)}, u32[]{:S(2)}, u32[]{:S(2)}) collective-permute-start(bf16[224,640]{1,0:T(8,128)(2,1)S(1)} %slice.122), channel_id=1, source_target_pairs={{0,16},{16,0},{1,17},{17,1},{2,18},{18,2},{3,19},{19,3},{4,20},{20... | collective-permute-start | bytes 860168 | tf_op jit(solution)/shard_map/ppermute | solution.py:32
  197.3 7.5 %collective-permute-done.30 = bf16[448,640]{1,0:T(8,128)(2,1)S(1)} collective-permute-done((bf16[448,640]{1,0:T(8,128)(2,1)}, bf16[448,640]{1,0:T(8,128)(2,1)S(1)}, u32[]{:S(2)}, u32[]{:S(2)}) %collective-permute-start.30) | collective-permute-done | bytes 573472 | tf_op jit(solution)/shard_map/ppermute | solution.py:32
  205.0 2.4 collective-permute-start.31
  208.1 5.6 %collective-permute-done.24 = bf16[224,1024]{1,0:T(8,128)(2,1)S(1)} collective-permute-done((bf16[224,1024]{1,0:T(8,128)(2,1)S(1)}, bf16[224,1024]{1,0:T(8,128)(2,1)S(1)}, u32[]{:S(2)}, u32[]{:S(2)}) %collective-permute-start.24) | collective-permute-done | bytes 458784 | tf_op jit(solution)/shard_map/ppermute | solution.py:32
  215.4 5.0 %collective-permute-done.31 = bf16[224,640]{1,0:T(8,128)(2,1)S(1)} collective-permute-done((bf16[224,640]{1,0:T(8,128)(2,1)S(1)}, bf16[224,640]{1,0:T(8,128)(2,1)S(1)}, u32[]{:S(2)}, u32[]{:S(2)}) %collective-permute-start.31) | collective-permute-done | bytes 286752 | tf_op jit(solution)/shard_map/ppermute | solution.py:32
  222.6 3.9 %all-to-all-start.5 = ((bf16[4,56,1920]{2,1,0:T(8,128)(2,1)}), bf16[4,56,1920]{2,1,0:T(8,128)(2,1)S(1)}, u32[]{:S(2)}, u32[]{:S(2)}) async-start(bf16[4,56,1920]{2,1,0:T(8,128)(2,1)} %bitcast.7), calls=%async_computation.5 | async-start | bytes 1720320 | tf_op jit(solution)/shard_map/all_to_all | solution.py:41
  226.6 2.1 collective-permute-start.26
  228.7 2.4 collective-permute-start.27
  231.9 2.3 shard_map.235
  234.1 9.1 %collective-permute-done.26 = bf16[56,1024]{1,0:T(8,128)(2,1)S(1)} collective-permute-done((bf16[56,1024]{1,0:T(8,128)(2,1)S(1)}, bf16[56,1024]{1,0:T(8,128)(2,1)S(1)}, u32[]{:S(2)}, u32[]{:S(2)}) %collective-permute-start.26) | collective-permute-done | bytes 114720 | tf_op jit(solution)/shard_map/ppermute | solution.py:620
  243.2 2.8 %collective-permute-done.28 = bf16[56,1024]{1,0:T(8,128)(2,1)S(1)} collective-permute-done((bf16[56,1024]{1,0:T(8,128)(2,1)S(1)}, bf16[56,1024]{1,0:T(8,128)(2,1)S(1)}, u32[]{:S(2)}, u32[]{:S(2)}) %collective-permute-start.28) | collective-permute-done | bytes 114720 | tf_op jit(solution)/shard_map/ppermute | solution.py:620
  247.8 3.2 %shard_map.234 = bf16[128,896]{1,0:T(8,128)(2,1)} custom-call(s32[2]{0:T(128)} %pad_add_fusion.s.refs_0_, bf16[4,128,896]{2,1,0:T(8,128)(2,1)} %copy-done.3, bf16[896,896]{1,0:T(8,128)(2,1)} %fusion.perm, f32[256,896]{1,0:T(8,128)} %get-tuple-element.100.refs_5_.mid), custom_call_target="tpu_custom_call" | custom-call | flops 1000 | bytes 1000 | tf_op jit(solution)/shard_map/pallas_call | solution.py:58
  (169 shorter events, 41.0 us)
Async XLA Ops:
  4.6 31.0 %all-to-all-start = ((bf16[4,56,1920]{2,1,0:T(8,128)(2,1)}), bf16[4,56,1920]{2,1,0:T(8,128)(2,1)S(1)}, u32[]{:S(2)}, u32[]{:S(2)}) async-start(bf16[4,56,1920]{2,1,0:T(8,128)(2,1)} %shard_map.224), calls=%async_computation | async-start | bytes 1720320 | tf_op jit(solution)/shard_map/all_to_all | solution.py:41
  9.8 16.5 %collective-permute-start.1 = (bf16[56,1024]{1,0:T(8,128)(2,1)S(1)}, bf16[56,1024]{1,0:T(8,128)(2,1)S(1)}, u32[]{:S(2)}, u32[]{:S(2)}) collective-permute-start(bf16[56,1024]{1,0:T(8,128)(2,1)S(1)} %copy-done.25), channel_id=1, source_target_pairs={{0,8},{8,0},{16,24},{24,16},{1,9},{9,1},{17,25},{25,17},{2,10},{10... | collective-permute-start | bytes 344072 | tf_op jit(solution)/shard_map/ppermute | solution.py:45
  11.9 14.5 %collective-permute-start.2 = (bf16[56,1024]{1,0:T(8,128)(2,1)S(1)}, bf16[56,1024]{1,0:T(8,128)(2,1)S(1)}, u32[]{:S(2)}, u32[]{:S(2)}) collective-permute-start(bf16[56,1024]{1,0:T(8,128)(2,1)S(1)} %copy-done.25), channel_id=1, source_target_pairs={{0,16},{8,24},{16,0},{24,8},{1,17},{9,25},{17,1},{25,9},{2,18},{10... | collective-permute-start | bytes 344072 | tf_op jit(solution)/shard_map/ppermute | solution.py:45
  14.4 16.4 %collective-permute-start.3 = (bf16[56,1024]{1,0:T(8,128)(2,1)S(1)}, bf16[56,1024]{1,0:T(8,128)(2,1)S(1)}, u32[]{:S(2)}, u32[]{:S(2)}) collective-permute-start(bf16[56,1024]{1,0:T(8,128)(2,1)S(1)} %copy-done.25), channel_id=1, source_target_pairs={{0,24},{8,16},{16,8},{24,0},{1,25},{9,17},{17,9},{25,1},{2,26},{10... | collective-permute-start | bytes 344072 | tf_op jit(solution)/shard_map/ppermute | solution.py:45
  14.5 18.9 %collective-permute-start = (bf16[128,896]{1,0:T(8,128)(2,1)S(1)}, bf16[128,896]{1,0:T(8,128)(2,1)S(1)}, u32[]{:S(2)}, u32[]{:S(2)}) collective-permute-start(bf16[128,896]{1,0:T(8,128)(2,1)S(1)} %copy-done.9), channel_id=1, source_target_pairs={{0,1},{1,0},{2,3},{3,2},{4,5},{5,4},{6,7},{7,6},{8,9},{9,8},{10,11... | collective-permute-start | bytes 688136 | tf_op jit(solution)/shard_map/ppermute | solution.py:32
  14.5 19.6 %collective-permute-start.4 = (bf16[128,896]{1,0:T(8,128)(2,1)S(1)}, bf16[128,896]{1,0:T(8,128)(2,1)S(1)}, u32[]{:S(2)}, u32[]{:S(2)}) collective-permute-start(bf16[128,896]{1,0:T(8,128)(2,1)S(1)} %copy-done.20), channel_id=1, source_target_pairs={{0,1},{1,0},{2,3},{3,2},{4,5},{5,4},{6,7},{7,6},{8,9},{9,8},{10,11... | collective-permute-start | bytes 688136 | tf_op jit(solution)/shard_map/ppermute | solution.py:32
  34.1 13.7 %collective-permute-start.6 = (bf16[224,1024]{1,0:T(8,128)(2,1)}, bf16[224,1024]{1,0:T(8,128)(2,1)S(1)}, u32[]{:S(2)}, u32[]{:S(2)}) collective-permute-start(bf16[224,1024]{1,0:T(8,128)(2,1)} %shard_map.223.refs_6_.refs_14_), channel_id=1, source_target_pairs={{0,4},{4,0},{1,5},{5,1},{2,6},{6,2},{3,7},{7,3},{8,12},{12,8},{9,1... | collective-permute-start | bytes 1376264 | tf_op jit(solution)/shard_map/ppermute | solution.py:32
  35.6 37.2 %copy-start.2 = (bf16[224,1280]{1,0:T(8,128)(2,1)}, bf16[224,1280]{1,0:T(8,128)(2,1)S(1)}, u32[]{:S(2)}) copy-start(bf16[224,1280]{1,0:T(8,128)(2,1)S(1)} %slice.109.refs_2_.refs_3_) | copy-start | bytes 1720324
  35.6 24.4 %collective-permute-start.8 = (bf16[224,1280]{1,0:T(8,128)(2,1)S(1)}, bf16[224,1280]{1,0:T(8,128)(2,1)S(1)}, u32[]{:S(2)}, u32[]{:S(2)}) collective-permute-start(bf16[224,1280]{1,0:T(8,128)(2,1)S(1)} %slice.109.refs_2_.refs_3_), channel_id=1, source_target_pairs={{0,16},{16,0},{1,17},{17,1},{2,18},{18,2},{3,19},{19,3},{4,20},{20... | collective-permute-start | bytes 1720328 | tf_op jit(solution)/shard_map/ppermute | solution.py:32
  35.7 24.4 %collective-permute-start.9 = (bf16[224,1280]{1,0:T(8,128)(2,1)S(1)}, bf16[224,1280]{1,0:T(8,128)(2,1)S(1)}, u32[]{:S(2)}, u32[]{:S(2)}) collective-permute-start(bf16[224,1280]{1,0:T(8,128)(2,1)S(1)} %slice.109.refs_2_.refs_3_), channel_id=1, source_target_pairs={{0,4},{4,0},{1,5},{5,1},{2,6},{6,2},{3,7},{7,3},{8,12},{12,8},{9,1... | collective-permute-start | bytes 1720328 | tf_op jit(solution)/shard_map/ppermute | solution.py:32
  36.5 12.7 %collective-permute-start.5 = (bf16[224,1024]{1,0:T(8,128)(2,1)}, bf16[224,1024]{1,0:T(8,128)(2,1)S(1)}, u32[]{:S(2)}, u32[]{:S(2)}) collective-permute-start(bf16[224,1024]{1,0:T(8,128)(2,1)} %shard_map.223.refs_6_.refs_14_), channel_id=1, source_target_pairs={{0,2},{2,0},{1,3},{3,1},{4,6},{6,4},{5,7},{7,5},{8,10},{10,8},{9,1... | collective-permute-start | bytes 1376264 | tf_op jit(solution)/shard_map/ppermute | solution.py:32
  47.7 9.3 %collective-permute-start.7 = (bf16[224,1024]{1,0:T(8,128)(2,1)S(1)}, bf16[224,1024]{1,0:T(8,128)(2,1)S(1)}, u32[]{:S(2)}, u32[]{:S(2)}) collective-permute-start(bf16[224,1024]{1,0:T(8,128)(2,1)S(1)} %collective-permute-done.6.refs_8_.refs_16_), channel_id=1, source_target_pairs={{0,2},{2,0},{1,3},{3,1},{4,6},{6,4},{5,7},{7,5},{8,10},{10,8},{9,1... | collective-permute-start | bytes 1376264 | tf_op jit(solution)/shard_map/ppermute | solution.py:32
  60.1 22.3 %all-to-all-start.1 = ((bf16[4,128,896]{2,1,0:T(8,128)(2,1)}), bf16[4,128,896]{2,1,0:T(8,128)(2,1)S(1)}, u32[]{:S(2)}, u32[]{:S(2)}) async-start(bf16[4,128,896]{2,1,0:T(8,128)(2,1)} %shard_map.221), calls=%async_computation.1 | async-start | bytes 1835008 | tf_op jit(solution)/shard_map/all_to_all | solution.py:41
  63.6 16.6 %collective-permute-start.12 = (bf16[224,1280]{1,0:T(8,128)(2,1)S(1)}, bf16[224,1280]{1,0:T(8,128)(2,1)}, u32[]{:S(2)}, u32[]{:S(2)}) collective-permute-start(bf16[224,1280]{1,0:T(8,128)(2,1)S(1)} %collective-permute-done.8.refs_3_.refs_4_), channel_id=1, source_target_pairs={{0,4},{4,0},{1,5},{5,1},{2,6},{6,2},{3,7},{7,3},{8,12},{12,8},{9,1... | collective-permute-start | bytes 1720328 | tf_op jit(solution)/shard_map/ppermute | solution.py:32
  64.7 26.6 %copy-start.6 = (bf16[224,640]{1,0:T(8,128)(2,1)}, bf16[224,640]{1,0:T(8,128)(2,1)S(1)}, u32[]{:S(2)}) copy-start(bf16[224,640]{1,0:T(8,128)(2,1)S(1)} %slice.110.refs_7_.refs_1_) | copy-start | bytes 860164
  64.7 15.6 %collective-permute-start.13 = (bf16[224,640]{1,0:T(8,128)(2,1)S(1)}, bf16[224,640]{1,0:T(8,128)(2,1)S(1)}, u32[]{:S(2)}, u32[]{:S(2)}) collective-permute-start(bf16[224,640]{1,0:T(8,128)(2,1)S(1)} %slice.110.refs_7_.refs_1_), channel_id=1, source_target_pairs={{0,16},{16,0},{1,17},{17,1},{2,18},{18,2},{3,19},{19,3},{4,20},{20... | collective-permute-start | bytes 860168 | tf_op jit(solution)/shard_map/ppermute | solution.py:32
  72.9 7.4 %collective-permute-start.10 = (bf16[128,896]{1,0:T(8,128)(2,1)}, bf16[128,896]{1,0:T(8,128)(2,1)S(1)}, u32[]{:S(2)}, u32[]{:S(2)}) collective-permute-start(bf16[128,896]{1,0:T(8,128)(2,1)} %get-tuple-element.75.top), channel_id=1, source_target_pairs={{0,1},{1,0},{2,3},{3,2},{4,5},{5,4},{6,7},{7,6},{8,9},{9,8},{10,11... | collective-permute-start | bytes 688136 | tf_op jit(solution)/shard_map/ppermute | solution.py:32
  73.0 7.3 %collective-permute-start.11 = (bf16[128,896]{1,0:T(8,128)(2,1)}, bf16[128,896]{1,0:T(8,128)(2,1)S(1)}, u32[]{:S(2)}, u32[]{:S(2)}) collective-permute-start(bf16[128,896]{1,0:T(8,128)(2,1)} %get-tuple-element.76.low), channel_id=1, source_target_pairs={{0,1},{1,0},{2,3},{3,2},{4,5},{5,4},{6,7},{7,6},{8,9},{9,8},{10,11... | collective-permute-start | bytes 688136 | tf_op jit(solution)/shard_map/ppermute | solution.py:32
  82.4 22.0 %copy-start = (bf16[4,128,896]{2,1,0:T(8,128)(2,1)}, bf16[4,128,896]{2,1,0:T(8,128)(2,1)S(1)}, u32[]{:S(2)}) copy-start(bf16[4,128,896]{2,1,0:T(8,128)(2,1)S(1)} %all-to-all-done.1.refs_0_) | copy-start | bytes 2752516
  86.5 17.8 %all-to-all-start.2 = ((bf16[4,128,896]{2,1,0:T(8,128)(2,1)}), bf16[4,128,896]{2,1,0:T(8,128)(2,1)S(1)}, u32[]{:S(2)}, u32[]{:S(2)}) async-start(bf16[4,128,896]{2,1,0:T(8,128)(2,1)} %get-tuple-element.79), calls=%async_computation.2 | async-start | bytes 1835008 | tf_op jit(solution)/shard_map/all_to_all | solution.py:41
  90.2 9.8 %collective-permute-start.15 = (bf16[224,640]{1,0:T(8,128)(2,1)S(1)}, bf16[224,640]{1,0:T(8,128)(2,1)S(1)}, u32[]{:S(2)}, u32[]{:S(2)}) collective-permute-start(bf16[224,640]{1,0:T(8,128)(2,1)S(1)} %collective-permute-done.13.refs_8_.refs_2_), channel_id=1, source_target_pairs={{0,4},{4,0},{1,5},{5,1},{2,6},{6,2},{3,7},{7,3},{8,12},{12,8},{9,1... | collective-permute-start | bytes 860168 | tf_op jit(solution)/shard_map/ppermute | solution.py:32
  91.2 13.1 %collective-permute-start.14 = (bf16[224,640]{1,0:T(8,128)(2,1)S(1)}, bf16[224,640]{1,0:T(8,128)(2,1)S(1)}, u32[]{:S(2)}, u32[]{:S(2)}) collective-permute-start(bf16[224,640]{1,0:T(8,128)(2,1)S(1)} %slice.110.refs_7_.refs_1_), channel_id=1, source_target_pairs={{0,4},{4,0},{1,5},{5,1},{2,6},{6,2},{3,7},{7,3},{8,12},{12,8},{9,1... | collective-permute-start | bytes 860168 | tf_op jit(solution)/shard_map/ppermute | solution.py:32
  100.1 22.9 %copy-start.14 = (bf16[224,640]{1,0:T(8,128)(2,1)}, bf16[224,640]{1,0:T(8,128)(2,1)S(1)}, u32[]{:S(2)}) copy-start(bf16[224,640]{1,0:T(8,128)(2,1)S(1)} %collective-permute-done.15.refs_10_.refs_4_) | copy-start | bytes 860164
  104.4 3.1 %collective-permute-start.16 = (bf16[4,128,896]{2,1,0:T(8,128)(2,1)S(1)}, bf16[4,128,896]{2,1,0:T(8,128)(2,1)}, u32[]{:S(2)}, u32[]{:S(2)}) collective-permute-start(bf16[4,128,896]{2,1,0:T(8,128)(2,1)S(1)} %all-to-all-done.2.refs_0_), channel_id=1, source_target_pairs={{0,1},{1,0},{2,3},{3,2},{4,5},{5,4},{6,7},{7,6},{8,9},{9,8},{10,11... | collective-permute-start | bytes 2752520 | tf_op jit(solution)/shard_map/ppermute | solution.py:32
  104.4 11.2 %collective-permute-start.17 = (bf16[4,128,896]{2,1,0:T(8,128)(2,1)S(1)}, bf16[4,128,896]{2,1,0:T(8,128)(2,1)S(1)}, u32[]{:S(2)}, u32[]{:S(2)}) collective-permute-start(bf16[4,128,896]{2,1,0:T(8,128)(2,1)S(1)} %all-to-all-done.1.refs_0_), channel_id=1, source_target_pairs={{0,1},{1,0},{2,3},{3,2},{4,5},{5,4},{6,7},{7,6},{8,9},{9,8},{10,11... | collective-permute-start | bytes 2752520 | tf_op jit(solution)/shard_map/ppermute | solution.py:32
  133.9 2.7 %collective-permute-start.18 = (bf16[4,128,896]{2,1,0:T(8,128)(2,1)}, bf16[4,128,896]{2,1,0:T(8,128)(2,1)S(1)}, u32[]{:S(2)}, u32[]{:S(2)}) collective-permute-start(bf16[4,128,896]{2,1,0:T(8,128)(2,1)} %get-tuple-element.90), channel_id=1, source_target_pairs={{0,1},{1,0},{2,3},{3,2},{4,5},{5,4},{6,7},{7,6},{8,9},{9,8},{10,11... | collective-permute-start | bytes 2752520 | tf_op jit(solution)/shard_map/ppermute | solution.py:32
  139.0 19.0 %all-to-all-start.3 = ((bf16[4,128,896]{2,1,0:T(8,128)(2,1)}), bf16[4,128,896]{2,1,0:T(8,128)(2,1)S(1)}, u32[]{:S(2)}, u32[]{:S(2)}) async-start(bf16[4,128,896]{2,1,0:T(8,128)(2,1)} %add_convert_fusion.1), calls=%async_computation.3 | async-start | bytes 1835008 | tf_op jit(solution)/shard_map/all_to_all | solution.py:41
  142.7 15.1 %collective-permute-start.20 = (bf16[448,640]{1,0:T(8,128)(2,1)S(1)}, bf16[448,640]{1,0:T(8,128)(2,1)S(1)}, u32[]{:S(2)}, u32[]{:S(2)}) collective-permute-start(bf16[448,640]{1,0:T(8,128)(2,1)S(1)} %copy-done.39), channel_id=1, source_target_pairs={{0,4},{4,0},{1,5},{5,1},{2,6},{6,2},{3,7},{7,3},{8,12},{12,8},{9,1... | collective-permute-start | bytes 1720328 | tf_op jit(solution)/shard_map/ppermute | solution.py:32
  157.8 23.9 %collective-permute-start.19 = (bf16[4,128,896]{2,1,0:T(8,128)(2,1)}, bf16[4,128,896]{2,1,0:T(8,128)(2,1)S(1)}, u32[]{:S(2)}, u32[]{:S(2)}) collective-permute-start(bf16[4,128,896]{2,1,0:T(8,128)(2,1)} %get-tuple-element.95), channel_id=1, source_target_pairs={{0,1},{1,0},{2,3},{3,2},{4,5},{5,4},{6,7},{7,6},{8,9},{9,8},{10,11... | collective-permute-start | bytes 2752520 | tf_op jit(solution)/shard_map/ppermute | solution.py:32
  161.9 1.8 collective-permute-start.21
  174.6 13.9 %collective-permute-start.23 = (bf16[224,1024]{1,0:T(8,128)(2,1)}, bf16[224,1024]{1,0:T(8,128)(2,1)}, u32[]{:S(2)}, u32[]{:S(2)}) collective-permute-start(bf16[224,1024]{1,0:T(8,128)(2,1)} %get-tuple-element.109), channel_id=1, source_target_pairs={{0,2},{2,0},{1,3},{3,1},{4,6},{6,4},{5,7},{7,5},{8,10},{10,8},{9,1... | collective-permute-start | bytes 1376264 | tf_op jit(solution)/shard_map/ppermute | solution.py:32
  176.5 16.0 %collective-permute-start.32 = (bf16[448,640]{1,0:T(8,128)(2,1)}, bf16[448,640]{1,0:T(8,128)(2,1)S(1)}, u32[]{:S(2)}, u32[]{:S(2)}) collective-permute-start(bf16[448,640]{1,0:T(8,128)(2,1)} %get-tuple-element.92), channel_id=1, source_target_pairs={{0,4},{4,0},{1,5},{5,1},{2,6},{6,2},{3,7},{7,3},{8,12},{12,8},{9,1... | collective-permute-start | bytes 1720328 | tf_op jit(solution)/shard_map/ppermute | solution.py:32
  178.3 35.7 %collective-permute-start.29 = (bf16[224,640]{1,0:T(8,128)(2,1)}, bf16[224,640]{1,0:T(8,128)(2,1)}, u32[]{:S(2)}, u32[]{:S(2)}) collective-permute-start(bf16[224,640]{1,0:T(8,128)(2,1)} %slice.120), channel_id=1, source_target_pairs={{0,16},{16,0},{1,17},{17,1},{2,18},{18,2},{3,19},{19,3},{4,20},{20... | collective-permute-start | bytes 860168 | tf_op jit(solution)/shard_map/ppermute | solution.py:32
  180.7 24.1 %collective-permute-start.30 = (bf16[448,640]{1,0:T(8,128)(2,1)}, bf16[448,640]{1,0:T(8,128)(2,1)S(1)}, u32[]{:S(2)}, u32[]{:S(2)}) collective-permute-start(bf16[448,640]{1,0:T(8,128)(2,1)} %get-tuple-element.116), channel_id=1, source_target_pairs={{0,4},{4,0},{1,5},{5,1},{2,6},{6,2},{3,7},{7,3},{8,12},{12,8},{9,1... | collective-permute-start | bytes 1720328 | tf_op jit(solution)/shard_map/ppermute | solution.py:32
  182.8 39.8 %all-to-all-start.4 = ((bf16[4,128,896]{2,1,0:T(8,128)(2,1)}), bf16[4,128,896]{2,1,0:T(8,128)(2,1)S(1)}, u32[]{:S(2)}, u32[]{:S(2)}) async-start(bf16[4,128,896]{2,1,0:T(8,128)(2,1)} %add_convert_fusion), calls=%async_computation.4 | async-start | bytes 1835008 | tf_op jit(solution)/shard_map/all_to_all | solution.py:41
  186.5 21.7 %collective-permute-start.22 = (bf16[224,1024]{1,0:T(8,128)(2,1)}, bf16[224,1024]{1,0:T(8,128)(2,1)S(1)}, u32[]{:S(2)}, u32[]{:S(2)}) collective-permute-start(bf16[224,1024]{1,0:T(8,128)(2,1)} %get-tuple-element.107), channel_id=1, source_target_pairs={{0,2},{2,0},{1,3},{3,1},{4,6},{6,4},{5,7},{7,5},{8,10},{10,8},{9,1... | collective-permute-start | bytes 1376264 | tf_op jit(solution)/shard_map/ppermute | solution.py:32
  189.8 23.9 %collective-permute-start.24 = (bf16[224,1024]{1,0:T(8,128)(2,1)S(1)}, bf16[224,1024]{1,0:T(8,128)(2,1)S(1)}, u32[]{:S(2)}, u32[]{:S(2)}) collective-permute-start(bf16[224,1024]{1,0:T(8,128)(2,1)S(1)} %add_convert_fusion.6), channel_id=1, source_target_pairs={{0,4},{4,0},{1,5},{5,1},{2,6},{6,2},{3,7},{7,3},{8,12},{12,8},{9,1... | collective-permute-start | bytes 1376264 | tf_op jit(solution)/shard_map/ppermute | solution.py:32
  192.7 21.1 %copy-start.24 = (bf16[224,1024]{1,0:T(8,128)(2,1)S(1)}, bf16[224,1024]{1,0:T(8,128)(2,1)}, u32[]{:S(2)}) copy-start(bf16[224,1024]{1,0:T(8,128)(2,1)} %get-tuple-element.106) | copy-start | bytes 1376260
  192.7 22.7 %collective-permute-start.33 = (bf16[224,640]{1,0:T(8,128)(2,1)S(1)}, bf16[224,640]{1,0:T(8,128)(2,1)S(1)}, u32[]{:S(2)}, u32[]{:S(2)}) collective-permute-start(bf16[224,640]{1,0:T(8,128)(2,1)S(1)} %slice.122), channel_id=1, source_target_pairs={{0,16},{16,0},{1,17},{17,1},{2,18},{18,2},{3,19},{19,3},{4,20},{20... | collective-permute-start | bytes 860168 | tf_op jit(solution)/shard_map/ppermute | solution.py:32
  205.0 15.4 %collective-permute-start.31 = (bf16[224,640]{1,0:T(8,128)(2,1)S(1)}, bf16[224,640]{1,0:T(8,128)(2,1)S(1)}, u32[]{:S(2)}, u32[]{:S(2)}) collective-permute-start(bf16[224,640]{1,0:T(8,128)(2,1)S(1)} %slice.121), channel_id=1, source_target_pairs={{0,16},{16,0},{1,17},{17,1},{2,18},{18,2},{3,19},{19,3},{4,20},{20... | collective-permute-start | bytes 860168 | tf_op jit(solution)/shard_map/ppermute | solution.py:32
  222.6 28.4 %all-to-all-start.5 = ((bf16[4,56,1920]{2,1,0:T(8,128)(2,1)}), bf16[4,56,1920]{2,1,0:T(8,128)(2,1)S(1)}, u32[]{:S(2)}, u32[]{:S(2)}) async-start(bf16[4,56,1920]{2,1,0:T(8,128)(2,1)} %bitcast.7), calls=%async_computation.5 | async-start | bytes 1720320 | tf_op jit(solution)/shard_map/all_to_all | solution.py:41
  226.5 19.6 %copy-start.36 = (bf16[56,64]{1,0:T(8,128)(2,1)S(1)}, bf16[56,64]{1,0:T(8,128)(2,1)}, u32[]{:S(2)}) copy-start(bf16[56,64]{1,0:T(8,128)(2,1)} %v.1) | copy-start | bytes 21508
  226.5 20.4 %copy-start.29 = (bf16[56,448]{1,0:T(8,128)(2,1)S(1)}, bf16[56,448]{1,0:T(8,128)(2,1)}, u32[]{:S(2)}) copy-start(bf16[56,448]{1,0:T(8,128)(2,1)} %q.1) | copy-start | bytes 150532
  226.5 4.6 %collective-permute-start.25 = (bf16[128,896]{1,0:T(8,128)(2,1)S(1)}, bf16[128,896]{1,0:T(8,128)(2,1)S(1)}, u32[]{:S(2)}, u32[]{:S(2)}) collective-permute-start(bf16[128,896]{1,0:T(8,128)(2,1)S(1)} %copy-done.40), channel_id=1, source_target_pairs={{0,1},{1,0},{2,3},{3,2},{4,5},{5,4},{6,7},{7,6},{8,9},{9,8},{10,11... | collective-permute-start | bytes 688136 | tf_op jit(solution)/shard_map/ppermute | solution.py:32
  226.6 16.6 %collective-permute-start.26 = (bf16[56,1024]{1,0:T(8,128)(2,1)S(1)}, bf16[56,1024]{1,0:T(8,128)(2,1)S(1)}, u32[]{:S(2)}, u32[]{:S(2)}) collective-permute-start(bf16[56,1024]{1,0:T(8,128)(2,1)S(1)} %get-tuple-element.128), channel_id=1, source_target_pairs={{0,8},{8,0},{16,24},{24,16},{1,9},{9,1},{17,25},{25,17},{2,10},{10... | collective-permute-start | bytes 344072 | tf_op jit(solution)/shard_map/ppermute | solution.py:620
  228.7 14.5 %collective-permute-start.27 = (bf16[56,1024]{1,0:T(8,128)(2,1)S(1)}, bf16[56,1024]{1,0:T(8,128)(2,1)S(1)}, u32[]{:S(2)}, u32[]{:S(2)}) collective-permute-start(bf16[56,1024]{1,0:T(8,128)(2,1)S(1)} %get-tuple-element.130), channel_id=1, source_target_pairs={{0,16},{8,24},{16,0},{24,8},{1,17},{9,25},{17,1},{25,9},{2,18},{10... | collective-permute-start | bytes 344072 | tf_op jit(solution)/shard_map/ppermute | solution.py:620
  231.1 14.9 %collective-permute-start.28 = (bf16[56,1024]{1,0:T(8,128)(2,1)S(1)}, bf16[56,1024]{1,0:T(8,128)(2,1)S(1)}, u32[]{:S(2)}, u32[]{:S(2)}) collective-permute-start(bf16[56,1024]{1,0:T(8,128)(2,1)S(1)} %get-tuple-element.129), channel_id=1, source_target_pairs={{0,24},{8,16},{16,8},{24,0},{1,25},{9,17},{17,9},{25,1},{2,26},{10... | collective-permute-start | bytes 344072 | tf_op jit(solution)/shard_map/ppermute | solution.py:620
  254.0 1.2 collective-permute-start.34
  (34 other events, 237.6 us)
